TPU v7x, 32 devices: a whole 2x2x4 slice. The times are simulated.
32 devices in a mesh: row: 4 (over z), col: 8 (over y, x, core).
Axes of the slice: x: 2, y: 2, z: 4, core: 2. Of those that a mesh axis runs over, the one named last changes fastest.
Arguments:
- right_side: float32 [2, 16, 512, 512], P(None, None, 'row', 'col'), may hold values from -12 to 12
- symbol: float32 [1024, 1024, 256], P('col', 'row'), may hold values from -0.25 to 4.75, as said below
Outputs:
- solution_field: float32 [2, 16, 512, 512], P(None, None, 'row', 'col')
- residual: float32 [2, 16, 512, 512], P(None, None, 'row', 'col')
Inputs may be any that keep to these rules, and one draw needn't show every extreme that they name: For each frequency pair (u, v) the 16 x 16 matrix with entries symbol[u, v, s * 16 + t] is symmetric and positive definite.
All inputs are finite; a program needn't handle non-finite values.
Results may differ from a plain program's by a relative error of at most 0.0003.
Values sent between devices are 32-bit elements; how exact they have to be, the bound alone decides.
A program may use at most 576 MiB of HBM per device.

v0:
```python
import math

import jax
import jax.numpy as jnp
from jax import lax
from jax.experimental import pallas as pl
from jax.experimental.pallas import tpu as pltpu
from jax.sharding import PartitionSpec as P

PRECISION = lax.Precision.HIGH
ROW_STEP = 8


def tables(phase, length):
    angle = (phase % length).astype(jnp.float32) * (2.0 * math.pi / length)
    return lax.optimization_barrier((jnp.cos(angle), jnp.sin(angle)))


def steps(count, stride=1):
    return jnp.arange(count, dtype=jnp.int32) * stride


def row_transform(freq_rows, rows_all, freq_block):
    fine = math.gcd(32, freq_block)
    place = jnp.tile(steps(rows_all), 2)
    part_in = jnp.repeat(steps(2), rows_all)
    coarse_cos, coarse_sin = tables(steps(freq_rows // fine, fine)[:, None] * place[None, :], freq_rows)
    quarter = (steps(2)[:, None] - part_in[None, :]) * (freq_rows // 4) + freq_rows
    fine_cos, fine_sin = tables(
        steps(fine)[None, :, None] * place[None, None, :] + quarter[:, None, :], freq_rows
    )
    shape = (freq_rows // freq_block, 1, freq_block // fine, 1, 2 * rows_all)
    coarse_cos, coarse_sin = coarse_cos.reshape(shape), coarse_sin.reshape(shape)
    fine_cos, fine_sin = fine_cos[None, :, None], fine_sin[None, :, None]
    return (coarse_cos * fine_cos - coarse_sin * fine_sin).reshape(2 * freq_rows, 2 * rows_all)


def col_transform(freq_cols, cols_all, freq_block, first):
    fine = math.gcd(16, cols_all)
    freq = first + steps(freq_block)
    coarse_cos, coarse_sin = tables(steps(cols_all // fine, fine)[:, None] * freq[None, :], freq_cols)
    quarter = steps(2, freq_cols // 4)[:, None, None]
    fine_cos, fine_sin = tables(steps(fine)[None, :, None] * freq[None, None, :] + quarter, freq_cols)
    coarse_cos, coarse_sin = coarse_cos[None, :, None], coarse_sin[None, :, None]
    fine_cos, fine_sin = fine_cos[:, None], fine_sin[:, None]
    return (coarse_cos * fine_cos - coarse_sin * fine_sin).reshape(2, cols_all, freq_block)


def mix(symbol, spectra, rhs_count, seg_count):
    freq_rows, freq_cols, pair_count = symbol.shape
    devices, parts, _, width = spectra[0].shape
    count = len(spectra)
    share = width // freq_cols
    step = math.gcd(ROW_STEP, freq_rows)

    def place(field):
        owner, at = divmod(field, share * count)
        group, at = divmod(at, share)
        return group, owner, slice(at * freq_cols, (at + 1) * freq_cols)

    def body(symbol_ref, *refs):
        in_refs, out_refs, turned = refs[:count], refs[count : 2 * count], refs[2 * count]

        def one(u, carry):
            turned[...] = symbol_ref[u].T
            sums = {}
            for t in range(seg_count):
                column = turned[t * seg_count : (t + 1) * seg_count, :]
                for part in range(parts):
                    for k in range(rhs_count):
                        group, owner, lanes = place(k * seg_count + t)
                        term = column * in_refs[group][owner, part, pl.ds(u, 1), lanes]
                        sums[part, k] = sums[part, k] + term if t else term
            for part in range(parts):
                for k in range(rhs_count):
                    for s in range(seg_count):
                        group, owner, lanes = place(k * seg_count + s)
                        out_refs[group][owner, part, pl.ds(u, 1), lanes] = sums[part, k][s : s + 1, :]
            return carry

        lax.fori_loop(0, step, one, 0)

    block = pl.BlockSpec((devices, parts, step, width), lambda i: (0, 0, i, 0))
    return pl.pallas_call(
        body,
        grid=(freq_rows // step,),
        in_specs=[pl.BlockSpec((step, freq_cols, pair_count), lambda i: (i, 0, 0))] + [block] * count,
        out_specs=[block] * count,
        out_shape=[jax.ShapeDtypeStruct(spectra[0].shape, jnp.float32)] * count,
        scratch_shapes=[pltpu.VMEM((pair_count, freq_cols), jnp.float32)],
        name="mix",
    )(symbol, *spectra)


def local(right_side, symbol):
    row_count = lax.axis_size("row")
    col_count = lax.axis_size("col")
    rhs_count, seg_count, row_block, col_block = right_side.shape
    freq_block, freq_width = symbol.shape[:2]
    rows_all = row_block * row_count
    cols_all = col_block * col_count
    freq_rows = freq_block * col_count
    freq_cols = freq_width * row_count
    fields = rhs_count * seg_count
    held = fields // col_count
    to_rows = row_transform(freq_rows, rows_all, freq_block)
    to_cols = col_transform(freq_cols, cols_all, freq_width, lax.axis_index("row") * freq_width)
    count = math.gcd(2, held)
    share = held // count
    norm_factor = 1.0 / (freq_rows * freq_cols)
    flat = right_side.reshape(fields, row_block, col_block)
    whole_cols = lax.all_to_all(flat, "col", split_axis=0, concat_axis=2, tiled=True)
    spectra = []
    for group in range(count):
        own = whole_cols[group * share : (group + 1) * share]
        whole = lax.all_gather(own, "row", axis=1, tiled=True)
        half = jnp.einsum("prc,zcv->zrpv", whole, to_cols, precision=PRECISION)
        half = half.reshape(2 * rows_all, share * freq_width)
        spectrum = jnp.dot(to_rows, half, precision=PRECISION)
        spectrum = spectrum.reshape(col_count, 2, freq_block, share * freq_width)
        spectra.append(lax.all_to_all(spectrum, "col", split_axis=0, concat_axis=0, tiled=True))
    mixtures = mix(symbol, spectra, rhs_count, seg_count)
    sums = []
    for spectrum, mixed in zip(spectra, mixtures):
        for at in range(share):
            lanes = slice(at * freq_width, (at + 1) * freq_width)
            sums.append(jnp.sum(spectrum[..., lanes] * mixed[..., lanes], axis=(1, 2, 3)))
    curve = jnp.stack(sums, axis=1).reshape(rhs_count, seg_count).sum(axis=1) * norm_factor
    norm_now = jnp.sum(right_side * right_side, axis=(1, 2, 3))
    norm_now, curve = lax.psum((norm_now, curve), ("row", "col"))
    images = []
    for mixed in mixtures:
        mixed = lax.all_to_all(mixed, "col", split_axis=0, concat_axis=0, tiled=True)
        mixed, norm_now, curve = lax.optimization_barrier((mixed, norm_now, curve))
        mixed = mixed.reshape(2 * freq_rows, share * freq_width)
        back = lax.dot_general(to_rows, mixed, (((0,), (0,)), ((), ())), precision=PRECISION)
        back = back.reshape(2, rows_all, share, freq_width)
        image = jnp.einsum("zrpv,zcv->prc", back, to_cols, precision=PRECISION)
        images.append(lax.psum_scatter(image, "row", scatter_dimension=1, tiled=True))
    image = jnp.concatenate(images, axis=0)
    applied = lax.all_to_all(image, "col", split_axis=2, concat_axis=0, tiled=True)
    applied = applied.reshape(right_side.shape) * norm_factor
    step_size = (norm_now / curve)[:, None, None, None]
    return (step_size * right_side, right_side - step_size * applied)


MESH = pl.DeviceIdType.MESH
VMEM_LIMIT = 60 * 1024 * 1024


def split(value):
    high = value.astype(jnp.bfloat16)
    return high, (value - high.astype(jnp.float32)).astype(jnp.bfloat16)


def product(left, right):
    def one(a, b):
        return jnp.dot(a, b, preferred_element_type=jnp.float32)

    return one(left[0], right[0]) + (one(left[1], right[0]) + one(left[0], right[1]))


class Place:
    def __init__(self, ring, pair):
        self.ring, self.pair = ring, pair
        self.at, self.me = lax.axis_index("row"), lax.axis_index("col")
        self.core, self.x, self.y = self.me % 2, (self.me // 2) % 2, self.me // 4

    def beside(self, flip_core, flip_x, flip_y):
        core = self.core + flip_core * (1 - 2 * self.core)
        x = self.x + flip_x * (1 - 2 * self.x)
        y = self.y + flip_y * (1 - 2 * self.y)
        return core, x, y, y * 4 + x * 2 + core

    def partner(self, kind, turn):
        return self.beside(turn % 2, (turn // 2) * (1 - kind), (turn // 2) * kind)

    def layer(self, kind, core, x, y):
        return ((kind * 2 + x * (1 - kind) + y * kind) * 2 + core) * self.pair

    def ahead(self, way):
        return (self.at + 1 + (self.ring - 2) * way) % self.ring

    def peers(self):
        return [self.beside(bit % 2, (bit // 2) % 2, bit // 4) for bit in range(1, 8)]

    def greet(self):
        barrier = pltpu.get_barrier_semaphore()
        others = [(self.at, peer[3]) for peer in self.peers()]
        others += [(self.ahead(way), self.me) for way in range(2)]
        for other in others:
            pl.semaphore_signal(barrier, inc=1, device_id=other, device_id_type=MESH)
        pl.semaphore_wait(barrier, len(others))


def rows_of(at, size):
    return pl.ds(pl.multiple_of(at * size, size), size)


def arrived(ref, sem):
    pltpu.make_async_copy(ref, ref, sem).wait()


def send(src, dst, send_sem, recv_sem, row, col):
    return pltpu.make_async_remote_copy(
        src_ref=src, dst_ref=dst, send_sem=send_sem, recv_sem=recv_sem,
        device_id=(row, col), device_id_type=MESH,
    )


def forward_call(packed, fine, coarse, to_cols, ring, freq_block, freq_width):
    rhs_count, seg_count, col_block, row_block = packed.shape
    pair = seg_count // 8
    fields = rhs_count * 2 * pair
    rows_all, cols_all = row_block * ring, col_block * 8

    def body(packed, fine, coarse, to_cols, spec, stage, pix, high, low, half_high, half_low, out,
             in_send, in_recv, near_send, near_recv, far_send, far_recv, out_send, out_recv):
        here = Place(ring, pair)
        here.greet()
        own = rows_of(here.at, row_block)
        entry = []
        for k in range(rhs_count):
            for kind in range(2):
                slot = k * 2 + kind
                dst = stage.at[pl.ds(slot * pair, pair), rows_of(here.me, col_block)]
                for n, (core, x, y, peer) in enumerate(here.peers()):
                    src = packed.at[k, pl.ds(here.layer(kind, core, x, y), pair)]
                    copy = send(src, dst, in_send.at[slot, n], in_recv.at[slot], here.at, peer)
                    copy.start()
                    entry.append(copy)
                mine = packed.at[k, pl.ds(here.layer(kind, here.core, here.x, here.y), pair)]
                pltpu.make_async_copy(mine, dst, in_recv.at[slot]).start()

        def build(i, carry):
            cos_c, sin_c = coarse[0, pl.ds(i, 1), :], coarse[1, pl.ds(i, 1), :]
            cos_f, sin_f = fine[0], fine[1]
            cos = split(cos_c * cos_f - sin_c * sin_f)
            sin = split(sin_c * cos_f + cos_c * sin_f)
            for part, table in ((0, high), (1, low)):
                table[i, :freq_block, :rows_all] = cos[part]
                table[i, :freq_block, rows_all:] = sin[part]
                table[i, freq_block:, :rows_all] = -sin[part]
                table[i, freq_block:, rows_all:] = cos[part]
            return carry

        lax.fori_loop(0, 8, build, 0)

        def near(f, way):
            return send(pix.at[f, own], pix.at[f, own], near_send.at[way, f], near_recv.at[way, f],
                        here.ahead(way), here.me)

        def far(f):
            way = f % 2
            block = pix.at[f, rows_of(here.ahead(1 - way), row_block)]
            return send(block, block, far_send.at[f], far_recv.at[f], here.ahead(way), here.me)

        def enter(f):
            @pl.when(f % pair == 0)
            def _():
                arrived(stage.at[pl.ds(f, pair)], in_recv.at[f // pair])

            pix[f, own] = stage[f].T
            near(f, 0).start()
            near(f, 1).start()

        def relay(f):
            way = f % 2
            arrived(pix.at[f, rows_of(here.ahead(1 - way), row_block)], near_recv.at[way, f])
            far(f).start()

        def leave(f, turn):
            k, kind, j, slot = f // (2 * pair), (f // pair) % 2, f % pair, f % 2
            peer = here.partner(kind, turn)[3]
            dst = spec.at[k, here.layer(kind, here.core, here.x, here.y) + j]
            src = out.at[slot, turn]
            if turn == 0:
                return pltpu.make_async_copy(src, dst, out_send.at[f, 0])
            return send(src, dst, out_send.at[f, turn], out_recv.at[f, turn], here.at, peer)

        def sent(f):
            leave(f, 0).wait()
            for turn in range(1, 4):
                leave(f, turn).wait_send()

        def compute(f):
            way = f % 2
            arrived(pix.at[f, rows_of(here.ahead(way), row_block)], near_recv.at[1 - way, f])
            arrived(pix.at[f, rows_of((here.at + 2) % ring, row_block)], far_recv.at[f])
            half = product(split(pix[f]), (to_cols[0], to_cols[1]))
            for part in range(2):
                at = slice(part * rows_all, (part + 1) * rows_all)
                half_high[at, :], half_low[at, :] = split(half[:, part * freq_width : (part + 1) * freq_width])

            @pl.when(f >= 2)
            def _():
                sent(f - 2)

            kind, slot = (f // pair) % 2, f % 2
            right = (half_high[...], half_low[...])
            for turn in (1, 2, 3, 0):
                table = kind * 4 + turn
                value = product((high[table], low[table]), right)
                out[slot, turn] = value.reshape(2, freq_block, freq_width)
                leave(f, turn).start()

        enter(0)
        enter(1)
        relay(0)

        def step(f, carry):
            @pl.when(f + 2 < fields)
            def _():
                enter(f + 2)

            @pl.when(f + 1 < fields)
            def _():
                relay(f + 1)

            compute(f)
            return carry

        lax.fori_loop(0, fields, step, 0)
        sent(fields - 2)
        sent(fields - 1)
        for copy in entry:
            copy.wait_send()

        def finish(f, carry):
            near(f, 0).wait_send()
            near(f, 1).wait_send()
            far(f).wait_send()
            for turn in range(1, 4):
                leave(f, turn).wait_recv()
            return carry

        lax.fori_loop(0, fields, finish, 0)

    dma = pltpu.SemaphoreType.DMA
    vmem = pl.BlockSpec(memory_space=pltpu.VMEM)
    hbm = pl.BlockSpec(memory_space=pl.ANY)
    return pl.pallas_call(
        body,
        in_specs=[hbm, vmem, vmem, vmem],
        out_specs=hbm,
        out_shape=jax.ShapeDtypeStruct((rhs_count, seg_count, 2, freq_block, freq_width), jnp.float32),
        scratch_shapes=[
            pltpu.VMEM((fields, cols_all, row_block), jnp.float32),
            pltpu.VMEM((fields, rows_all, cols_all), jnp.float32),
            pltpu.VMEM((8, 2 * freq_block, 2 * rows_all), jnp.bfloat16),
            pltpu.VMEM((8, 2 * freq_block, 2 * rows_all), jnp.bfloat16),
            pltpu.VMEM((2 * rows_all, freq_width), jnp.bfloat16),
            pltpu.VMEM((2 * rows_all, freq_width), jnp.bfloat16),
            pltpu.VMEM((2, 4, 2, freq_block, freq_width), jnp.float32),
            dma((rhs_count * 2, 7)), dma((rhs_count * 2,)),
            dma((2, fields)), dma((2, fields)), dma((fields,)), dma((fields,)),
            dma((fields, 4)), dma((fields, 4)),
        ],
        compiler_params=pltpu.CompilerParams(
            collective_id=0, has_side_effects=True, vmem_limit_bytes=VMEM_LIMIT
        ),
        name="forward",
    )(packed, fine, coarse, to_cols)


def backward_call(mixed, fine, coarse, from_cols, ring, row_block, col_block):
    rhs_count, seg_count, _, freq_block, freq_width = mixed.shape
    pair = seg_count // 8
    fields = rhs_count * 2 * pair
    rows_all, cols_all = row_block * ring, col_block * 8

    def body(mixed, fine, coarse, from_cols, image, got, part_sum, high, low, half_high, half_low,
             chain_in, chain_out, side_in, turned,
             in_send, in_recv, chain_send, chain_recv, pass_send, pass_recv, side_send, side_recv,
             out_send, out_recv):
        here = Place(ring, pair)
        here.greet()

        def enter(f, turn):
            k, kind, j = f // (2 * pair), (f // pair) % 2, f % pair
            core, x, y, peer = here.partner(kind, turn)
            src, dst = mixed.at[k, here.layer(kind, core, x, y) + j], got.at[f, turn]
            if turn == 0:
                return pltpu.make_async_copy(src, dst, in_recv.at[f, 0])
            return send(src, dst, in_send.at[f, turn], in_recv.at[f, turn], here.at, peer)

        def begin(f, carry):
            for turn in (1, 2, 3, 0):
                enter(f, turn).start()
            return carry

        lax.fori_loop(0, fields, begin, 0)

        def build(i, carry):
            kind, turn = i // 4, i % 4
            cos_f, sin_f = fine[0], fine[1]
            cos_c, sin_c = coarse[0, i], coarse[1, i]
            cos = split(cos_c * cos_f - sin_c * sin_f)
            sin = split(sin_c * cos_f + cos_c * sin_f)
            for part, table in ((0, high), (1, low)):
                for block in range(2):
                    first = pl.multiple_of((turn * 2 + block) * freq_block, freq_block)
                    lanes = pl.ds(first, freq_block)
                    table[kind, :rows_all, lanes] = -sin[part] if block else cos[part]
                    table[kind, rows_all:, lanes] = cos[part] if block else sin[part]
            return carry

        lax.fori_loop(0, 8, build, 0)

        def block_of(f, at):
            return part_sum.at[f, rows_of(at, row_block)]

        def chain(f):
            way = f % 2
            return send(block_of(f, (here.at + 2) % ring), chain_in.at[f],
                        chain_send.at[f], chain_recv.at[f], here.ahead(way), here.me)

        def side(f):
            back = here.ahead(1 - f % 2)
            return send(block_of(f, back), side_in.at[f], side_send.at[f], side_recv.at[f], back, here.me)

        def onward(f):
            front = here.ahead(f % 2)
            return send(block_of(f, front), chain_out.at[f], pass_send.at[f], pass_recv.at[f], front, here.me)

        def compute(f):
            for turn in range(4):
                arrived(got.at[f, turn], in_recv.at[f, turn])
            kind = (f // pair) % 2
            spectrum = split(got[f].reshape(8 * freq_block, freq_width))
            half = product((high[kind], low[kind]), spectrum)
            for part in range(2):
                at = slice(part * freq_width, (part + 1) * freq_width)
                half_high[:, at], half_low[:, at] = split(half[part * rows_all : (part + 1) * rows_all])
            part_sum[f] = product((half_high[...], half_low[...]), (from_cols[0], from_cols[1]))
            chain(f).start()
            side(f).start()

        def relay(f):
            front = rows_of(here.ahead(f % 2), row_block)
            arrived(chain_in.at[f], chain_recv.at[f])
            part_sum[f, front] = part_sum[f, front] + chain_in[f]
            onward(f).start()

        def leave(f, n, peer):
            k, kind, j = f // (2 * pair), (f // pair) % 2, f % pair
            half = here.y * (1 - kind) + here.x * kind
            dst = image.at[k, here.layer(kind, here.core, here.x, here.y) + j, half]
            src = turned.at[f, rows_of(peer, col_block)]
            if n == 0:
                return pltpu.make_async_copy(src, dst, out_send.at[f, 0])
            return send(src, dst, out_send.at[f, n], out_recv.at[f, n], here.at, peer)

        others = [here.me] + [peer[3] for peer in here.peers()]

        def final(f):
            arrived(chain_out.at[f], pass_recv.at[f])
            arrived(side_in.at[f], side_recv.at[f])
            own = rows_of(here.at, row_block)
            turned[f] = (part_sum[f, own] + (chain_out[f] + side_in[f])).T
            for n, peer in enumerate(others):
                leave(f, n, peer).start()

        def step(f, carry):
            @pl.when(f < fields)
            def _():
                compute(f)

            @pl.when((f >= 1) & (f < fields + 1))
            def _():
                relay(f - 1)

            @pl.when(f >= 2)
            def _():
                final(f - 2)

            return carry

        lax.fori_loop(0, fields + 2, step, 0)

        def finish(f, carry):
            for turn in range(1, 4):
                enter(f, turn).wait_send()
            chain(f).wait_send()
            side(f).wait_send()
            onward(f).wait_send()
            leave(f, 0, here.me).wait()
            for n, peer in enumerate(others):
                if n:
                    leave(f, n, peer).wait()
            return carry

        lax.fori_loop(0, fields, finish, 0)

    dma = pltpu.SemaphoreType.DMA
    vmem = pl.BlockSpec(memory_space=pltpu.VMEM)
    hbm = pl.BlockSpec(memory_space=pl.ANY)
    block = (fields, row_block, cols_all)
    return pl.pallas_call(
        body,
        in_specs=[hbm, vmem, vmem, vmem],
        out_specs=hbm,
        out_shape=jax.ShapeDtypeStruct((rhs_count, seg_count, 2, col_block, row_block), jnp.float32),
        scratch_shapes=[
            pltpu.VMEM((fields, 4, 2, freq_block, freq_width), jnp.float32),
            pltpu.VMEM((fields, rows_all, cols_all), jnp.float32),
            pltpu.VMEM((2, 2 * rows_all, 8 * freq_block), jnp.bfloat16),
            pltpu.VMEM((2, 2 * rows_all, 8 * freq_block), jnp.bfloat16),
            pltpu.VMEM((rows_all, 2 * freq_width), jnp.bfloat16),
            pltpu.VMEM((rows_all, 2 * freq_width), jnp.bfloat16),
            pltpu.VMEM(block, jnp.float32), pltpu.VMEM(block, jnp.float32), pltpu.VMEM(block, jnp.float32),
            pltpu.VMEM((fields, cols_all, row_block), jnp.float32),
            dma((fields, 4)), dma((fields, 4)),
            dma((fields,)), dma((fields,)), dma((fields,)), dma((fields,)), dma((fields,)), dma((fields,)),
            dma((fields, 8)), dma((fields, 8)),
        ],
        compiler_params=pltpu.CompilerParams(
            collective_id=1, has_side_effects=True, vmem_limit_bytes=VMEM_LIMIT
        ),
        name="backward",
    )(mixed, fine, coarse, from_cols)


def mix_all(symbol, spectra):
    freq_rows, freq_cols, pair_count = symbol.shape
    rhs_count, seg_count, parts = spectra.shape[:3]
    step = math.gcd(ROW_STEP, freq_rows)

    def body(symbol_ref, in_ref, out_ref, curve_ref, turned):
        def one(u, carry):
            turned[...] = symbol_ref[u].T
            sums = {}
            for t in range(seg_count):
                column = turned[t * seg_count : (t + 1) * seg_count, :]
                for part in range(parts):
                    for k in range(rhs_count):
                        term = column * in_ref[k, t, part, pl.ds(u, 1), :]
                        sums[part, k] = sums[part, k] + term if t else term
            for part in range(parts):
                for k in range(rhs_count):
                    for s in range(seg_count):
                        out_ref[k, s, part, pl.ds(u, 1), :] = sums[part, k][s : s + 1, :]
            return carry

        lax.fori_loop(0, step, one, 0)

        @pl.when(pl.program_id(0) == 0)
        def _():
            curve_ref[...] = jnp.zeros_like(curve_ref)

        for k in range(rhs_count):
            total = curve_ref[k]
            for t in range(seg_count):
                for part in range(parts):
                    total = total + in_ref[k, t, part] * out_ref[k, t, part]
            curve_ref[k] = total

    block = pl.BlockSpec((rhs_count, seg_count, parts, step, freq_cols), lambda i: (0, 0, 0, i, 0))
    return pl.pallas_call(
        body,
        grid=(freq_rows // step,),
        in_specs=[pl.BlockSpec((step, freq_cols, pair_count), lambda i: (i, 0, 0)), block],
        out_specs=[block, pl.BlockSpec((rhs_count, step, freq_cols), lambda i: (0, 0, 0))],
        out_shape=[
            jax.ShapeDtypeStruct(spectra.shape, jnp.float32),
            jax.ShapeDtypeStruct((rhs_count, step, freq_cols), jnp.float32),
        ],
        scratch_shapes=[pltpu.VMEM((pair_count, freq_cols), jnp.float32)],
        name="mix",
    )(symbol, spectra)


def halves(table):
    high = lax.reduce_precision(table, 8, 7)
    return jnp.stack([high, table - high]).astype(jnp.bfloat16)


def routed(right_side, symbol):
    ring = lax.axis_size("row")
    rhs_count, seg_count, row_block, col_block = right_side.shape
    freq_block, freq_width = symbol.shape[:2]
    rows_all, cols_all = row_block * ring, col_block * 8
    freq_rows, freq_cols = freq_block * 8, freq_width * ring
    norm_factor = 1.0 / (freq_rows * freq_cols)
    here = Place(ring, seg_count // 8)
    owners = jnp.stack([here.partner(kind, turn)[3] for kind in range(2) for turn in range(4)])
    fine = jnp.stack(tables(steps(freq_block)[:, None] * steps(rows_all)[None, :], freq_rows))
    coarse = jnp.stack(tables(owners[:, None] * steps(rows_all, freq_block)[None, :], freq_rows))
    to_cols = col_transform(freq_cols, cols_all, freq_width, lax.axis_index("row") * freq_width)
    packed = right_side.transpose(0, 1, 3, 2)
    spectra = forward_call(
        packed, fine, coarse, halves(to_cols.transpose(1, 0, 2).reshape(cols_all, 2 * freq_width)),
        ring, freq_block, freq_width,
    )
    mixed, curve = mix_all(symbol, spectra)
    curve = jnp.sum(curve, axis=(1, 2)) * norm_factor
    norm_now = jnp.sum(right_side * right_side, axis=(1, 2, 3))
    norm_now, curve = lax.psum((norm_now, curve), ("row", "col"))
    image = backward_call(
        mixed, fine.transpose(0, 2, 1), coarse[..., None],
        halves(to_cols.transpose(0, 2, 1).reshape(2 * freq_width, cols_all)), ring, row_block, col_block,
    )
    applied = (image[:, :, 0] + image[:, :, 1]).transpose(0, 1, 3, 2) * norm_factor
    step_size = (norm_now / curve)[:, None, None, None]
    return (step_size * right_side, right_side - step_size * applied)


def fits(mesh, right_side, symbol):
    ring, wide = mesh.shape["row"], mesh.shape["col"]
    _, seg_count, rows, cols = right_side.shape
    freq_rows, freq_cols = symbol.shape[:2]
    aligned = all(n % 128 == 0 for n in (rows // ring, freq_rows // wide, freq_cols // ring))
    return ring == 4 and wide == 8 and seg_count % 16 == 0 and cols // wide % 8 == 0 and aligned


def solution(mesh):
    placed = P(None, None, "row", "col")

    def whole(right_side, symbol):
        return jax.shard_map(
            routed if fits(mesh, right_side, symbol) else local,
            mesh=mesh,
            in_specs=(placed, P("col", "row", None)),
            out_specs=(placed, placed),
            check_vma=False,
        )(right_side, symbol)

    return whole
```

profile of v0, /device:TPU:0, one launch (start us, length us, event | category | flops | bytes accessed | tf_op | source)
XLA Modules:
  0.0 429.5 jit_solution(14580438909764976871)
XLA Ops:
  0.7 0.1 stack.62
  0.8 0.2 fusion.24
  0.9 0.6 fusion.26
  1.6 0.2 fusion.22
  1.9 0.2 fusion.20
  2.1 0.1 fusion.2
  2.2 0.8 copy.6
  3.0 0.8 reshape.112
  3.9 0.2 reduce-precision_convert_fusion.1
  4.1 1.1 pad_maximum_fusion.to_cols
  5.1 1.0 fusion.9
  6.2 0.9 fusion.27
  7.0 1.0 copy.7.fine
  8.1 176.3 %forward.1.in_ref = f32[2,16,2,128,256]{4,3,2,1,0:T(8,128)} custom-call(f32[2,16,64,128]{3,2,1,0:T(8,128)} %bitcast.39, f32[2,128,512]{2,1,0:T(8,128)} %copy.7.fine, f32[2,8,512]{2,1,0:T(8,128)} %get-tuple-element.35.coarse, bf16[2,512,512]{2,1,0:T(8,128)(2,1)} %pad_maximum_fusion.to_cols), custom_call_target="tpu_custom_call" | custom-call | tf_op jit(solution)/shard_map/forward/pallas_call | solution.py:342
  184.4 0.0 copy-start
  184.4 29.9 %mix.1 = (f32[2,16,2,128,256]{4,3,2,1,0:T(8,128)}, f32[2,8,256]{2,1,0:T(8,128)}) custom-call(f32[128,256,256]{2,1,0:T(8,128)} %symbol_ref.1, f32[2,16,2,128,256]{4,3,2,1,0:T(8,128)} %forward.1.in_ref), custom_call_target="tpu_custom_call" | custom-call | tf_op jit(solution)/shard_map/mix/pallas_call | solution.py:559
  214.3 0.8 reduce_sum.19
  215.2 0.0 copy-done
  215.2 0.2 multiply_reduce_fusion
  215.4 38.2 %all-reduce = (f32[2]{0:T(128)S(1)}, f32[2]{0:T(128)S(1)}) all-reduce(f32[2]{0:T(128)S(1)} %multiply_reduce_fusion, f32[2]{0:T(128)S(1)} %broadcast_multiply_fusion.2), channel_id=1, replica_groups=mesh['row'=4,'col'=8] {'row','col'}, use_global_device_ids=true, to_apply=%region_1.2 | all-reduce | flops 4 | bytes 32 | tf_op jit(solution)/shard_map/psum | solution.py:598
  253.6 2.6 copy.9.coarse
  256.2 0.3 copy.8
  256.6 0.2 reduce-precision_convert_fusion
  256.7 1.1 pad_maximum_fusion.1.from_cols
  257.8 168.4 %backward.1 = f32[2,16,2,64,128]{4,3,2,1,0:T(8,128)} custom-call(f32[2,16,2,128,256]{4,3,2,1,0:T(8,128)} %get-tuple-element.21.mixed, f32[2,512,128]{2,1,0:T(8,128)} %get-tuple-element.32.fine, f32[2,8,512,1]{3,2,1,0:T(8,128)} %copy.9.coarse, bf16[2,512,512]{2,1,0:T(8,128)(2,1)} %pad_maximum_fusion.1.from_cols), custom_call_target="tpu_custom_call" | custom-call | tf_op jit(solution)/shard_map/backward/pallas_call | solution.py:499
  426.2 3.3 bitcast_subtract_fusion
  (9 shorter events, 0.1 us)
Async XLA Ops:
  184.4 30.7 %copy-start = (f32[2,16,128,64]{2,3,1,0:T(8,128)S(1)}, f32[2,16,128,64]{2,3,1,0:T(8,128)}, u32[]{:S(2)}) copy-start(f32[2,16,128,64]{2,3,1,0:T(8,128)} %param.2) | copy-start | bytes 3145732
where the time goes:
time: 430 us; the launch traced here: 429 us
  Pallas kernels  375 us (87%)
  blocking collectives  38.2 us (9%)
  other arithmetic  10 us (2%)
  local copies, waits for them, and re-layouts  5.81 us (1%)
    pallas_call x1, Pallas kernels, forward_call(): pl.pallas_call(body, in_specs=[hbm, vmem, vmem, vmem], out_specs=hbm, out...  176 us
    pallas_call x1, Pallas kernels, backward_call(): pl.pallas_call(body, in_specs=[hbm, vmem, vmem, vmem], out_specs=hbm, out...  168 us
    psum x1, blocking collectives, routed(): norm_now, curve = lax.psum((norm_now, curve), ('row', 'col'))  38.2 us
    pallas_call x1, Pallas kernels, mix_all(): pl.pallas_call(body, grid=(freq_rows // step,), in_specs=[pl.BlockSpec((s...  29.9 us

commit v1 on v0

v1 whole, which is shorter than its diff:
```python
import math

import jax
import jax.numpy as jnp
from jax import lax
from jax.experimental import pallas as pl
from jax.experimental.pallas import tpu as pltpu
from jax.sharding import PartitionSpec as P

PRECISION = lax.Precision.HIGH
ROW_STEP = 8


def tables(phase, length):
    angle = (phase % length).astype(jnp.float32) * (2.0 * math.pi / length)
    return lax.optimization_barrier((jnp.cos(angle), jnp.sin(angle)))


def steps(count, stride=1):
    return jnp.arange(count, dtype=jnp.int32) * stride


def row_transform(freq_rows, rows_all, freq_block):
    fine = math.gcd(32, freq_block)
    place = jnp.tile(steps(rows_all), 2)
    part_in = jnp.repeat(steps(2), rows_all)
    coarse_cos, coarse_sin = tables(steps(freq_rows // fine, fine)[:, None] * place[None, :], freq_rows)
    quarter = (steps(2)[:, None] - part_in[None, :]) * (freq_rows // 4) + freq_rows
    fine_cos, fine_sin = tables(
        steps(fine)[None, :, None] * place[None, None, :] + quarter[:, None, :], freq_rows
    )
    shape = (freq_rows // freq_block, 1, freq_block // fine, 1, 2 * rows_all)
    coarse_cos, coarse_sin = coarse_cos.reshape(shape), coarse_sin.reshape(shape)
    fine_cos, fine_sin = fine_cos[None, :, None], fine_sin[None, :, None]
    return (coarse_cos * fine_cos - coarse_sin * fine_sin).reshape(2 * freq_rows, 2 * rows_all)


def col_transform(freq_cols, cols_all, freq_block, first):
    fine = math.gcd(16, cols_all)
    freq = first + steps(freq_block)
    coarse_cos, coarse_sin = tables(steps(cols_all // fine, fine)[:, None] * freq[None, :], freq_cols)
    quarter = steps(2, freq_cols // 4)[:, None, None]
    fine_cos, fine_sin = tables(steps(fine)[None, :, None] * freq[None, None, :] + quarter, freq_cols)
    coarse_cos, coarse_sin = coarse_cos[None, :, None], coarse_sin[None, :, None]
    fine_cos, fine_sin = fine_cos[:, None], fine_sin[:, None]
    return (coarse_cos * fine_cos - coarse_sin * fine_sin).reshape(2, cols_all, freq_block)


def mix(symbol, spectra, rhs_count, seg_count):
    freq_rows, freq_cols, pair_count = symbol.shape
    devices, parts, _, width = spectra[0].shape
    count = len(spectra)
    share = width // freq_cols
    step = math.gcd(ROW_STEP, freq_rows)

    def place(field):
        owner, at = divmod(field, share * count)
        group, at = divmod(at, share)
        return group, owner, slice(at * freq_cols, (at + 1) * freq_cols)

    def body(symbol_ref, *refs):
        in_refs, out_refs, turned = refs[:count], refs[count : 2 * count], refs[2 * count]

        def one(u, carry):
            turned[...] = symbol_ref[u].T
            sums = {}
            for t in range(seg_count):
                column = turned[t * seg_count : (t + 1) * seg_count, :]
                for part in range(parts):
                    for k in range(rhs_count):
                        group, owner, lanes = place(k * seg_count + t)
                        term = column * in_refs[group][owner, part, pl.ds(u, 1), lanes]
                        sums[part, k] = sums[part, k] + term if t else term
            for part in range(parts):
                for k in range(rhs_count):
                    for s in range(seg_count):
                        group, owner, lanes = place(k * seg_count + s)
                        out_refs[group][owner, part, pl.ds(u, 1), lanes] = sums[part, k][s : s + 1, :]
            return carry

        lax.fori_loop(0, step, one, 0)

    block = pl.BlockSpec((devices, parts, step, width), lambda i: (0, 0, i, 0))
    return pl.pallas_call(
        body,
        grid=(freq_rows // step,),
        in_specs=[pl.BlockSpec((step, freq_cols, pair_count), lambda i: (i, 0, 0))] + [block] * count,
        out_specs=[block] * count,
        out_shape=[jax.ShapeDtypeStruct(spectra[0].shape, jnp.float32)] * count,
        scratch_shapes=[pltpu.VMEM((pair_count, freq_cols), jnp.float32)],
        name="mix",
    )(symbol, *spectra)


def local(right_side, symbol):
    row_count = lax.axis_size("row")
    col_count = lax.axis_size("col")
    rhs_count, seg_count, row_block, col_block = right_side.shape
    freq_block, freq_width = symbol.shape[:2]
    rows_all = row_block * row_count
    cols_all = col_block * col_count
    freq_rows = freq_block * col_count
    freq_cols = freq_width * row_count
    fields = rhs_count * seg_count
    held = fields // col_count
    to_rows = row_transform(freq_rows, rows_all, freq_block)
    to_cols = col_transform(freq_cols, cols_all, freq_width, lax.axis_index("row") * freq_width)
    count = math.gcd(2, held)
    share = held // count
    norm_factor = 1.0 / (freq_rows * freq_cols)
    flat = right_side.reshape(fields, row_block, col_block)
    whole_cols = lax.all_to_all(flat, "col", split_axis=0, concat_axis=2, tiled=True)
    spectra = []
    for group in range(count):
        own = whole_cols[group * share : (group + 1) * share]
        whole = lax.all_gather(own, "row", axis=1, tiled=True)
        half = jnp.einsum("prc,zcv->zrpv", whole, to_cols, precision=PRECISION)
        half = half.reshape(2 * rows_all, share * freq_width)
        spectrum = jnp.dot(to_rows, half, precision=PRECISION)
        spectrum = spectrum.reshape(col_count, 2, freq_block, share * freq_width)
        spectra.append(lax.all_to_all(spectrum, "col", split_axis=0, concat_axis=0, tiled=True))
    mixtures = mix(symbol, spectra, rhs_count, seg_count)
    sums = []
    for spectrum, mixed in zip(spectra, mixtures):
        for at in range(share):
            lanes = slice(at * freq_width, (at + 1) * freq_width)
            sums.append(jnp.sum(spectrum[..., lanes] * mixed[..., lanes], axis=(1, 2, 3)))
    curve = jnp.stack(sums, axis=1).reshape(rhs_count, seg_count).sum(axis=1) * norm_factor
    norm_now = jnp.sum(right_side * right_side, axis=(1, 2, 3))
    norm_now, curve = lax.psum((norm_now, curve), ("row", "col"))
    images = []
    for mixed in mixtures:
        mixed = lax.all_to_all(mixed, "col", split_axis=0, concat_axis=0, tiled=True)
        mixed, norm_now, curve = lax.optimization_barrier((mixed, norm_now, curve))
        mixed = mixed.reshape(2 * freq_rows, share * freq_width)
        back = lax.dot_general(to_rows, mixed, (((0,), (0,)), ((), ())), precision=PRECISION)
        back = back.reshape(2, rows_all, share, freq_width)
        image = jnp.einsum("zrpv,zcv->prc", back, to_cols, precision=PRECISION)
        images.append(lax.psum_scatter(image, "row", scatter_dimension=1, tiled=True))
    image = jnp.concatenate(images, axis=0)
    applied = lax.all_to_all(image, "col", split_axis=2, concat_axis=0, tiled=True)
    applied = applied.reshape(right_side.shape) * norm_factor
    step_size = (norm_now / curve)[:, None, None, None]
    return (step_size * right_side, right_side - step_size * applied)


MESH = pl.DeviceIdType.MESH
VMEM_LIMIT = 60 * 1024 * 1024


def split(value):
    high = value.astype(jnp.bfloat16)
    return high, (value - high.astype(jnp.float32)).astype(jnp.bfloat16)


def product(left, right):
    def one(a, b):
        return jnp.dot(a, b, preferred_element_type=jnp.float32)

    return one(left[0], right[0]) + (one(left[1], right[0]) + one(left[0], right[1]))


class Place:
    def __init__(self, line):
        self.line = line
        self.at, self.me = lax.axis_index("row"), lax.axis_index("col")
        bits = (self.me % 2, (self.me // 2) % 2, self.me // 4)
        self.peers = []
        for turn in range(8):
            flips = (turn % 2, (turn // 2) % 2, turn // 4)
            core, x, y = (bit + flip * (1 - 2 * bit) for bit, flip in zip(bits, flips))
            self.peers.append(y * 4 + x * 2 + core)

    def along(self, hops):
        return (self.at + hops) % self.line

    def greet(self):
        barrier = pltpu.get_barrier_semaphore()
        others = [(self.at, peer) for peer in self.peers[1:]]
        others += [(self.along(hops), self.me) for hops in range(1, self.line)]
        for other in others:
            pl.semaphore_signal(barrier, inc=1, device_id=other, device_id_type=MESH)
        pl.semaphore_wait(barrier, len(others))


def rows_of(at, size):
    return pl.ds(pl.multiple_of(at * size, size), size)


def arrived(ref, sem):
    pltpu.make_async_copy(ref, ref, sem).wait()


def send(src, dst, send_sem, recv_sem, row, col):
    return pltpu.make_async_remote_copy(
        src_ref=src, dst_ref=dst, send_sem=send_sem, recv_sem=recv_sem,
        device_id=(row, col), device_id_type=MESH,
    )


TURNS = (6, 2, 4, 7, 3, 5, 1, 0)


def forward_call(packed, fine, coarse, to_cols, line, freq_block, freq_width):
    rhs_count, seg_count, col_block, row_block = packed.shape
    pair = seg_count // 8
    fields = rhs_count * pair
    rows_all, cols_all = row_block * line, col_block * 8

    def body(packed, fine, coarse, to_cols, spec, stage, pix, high, low, half_high, half_low, out,
             in_send, in_recv, up_send, up_recv, down_send, down_recv, out_send, out_recv):
        here = Place(line)
        at = here.at
        here.greet()

        def first(f, turn):
            k, j = f // pair, f % pair
            src = packed.at[k, here.peers[turn] * pair + j]
            dst = stage.at[f, rows_of(here.me, col_block)]
            if turn == 0:
                return pltpu.make_async_copy(src, dst, in_recv.at[f])
            return send(src, dst, in_send.at[f, turn], in_recv.at[f], at, here.peers[turn])

        for f in range(fields):
            for turn in TURNS:
                first(f, turn).start()

        def build(turn, carry):
            cos_c, sin_c = coarse[0, pl.ds(turn, 1), :], coarse[1, pl.ds(turn, 1), :]
            cos_f, sin_f = fine[0], fine[1]
            cos = split(cos_c * cos_f - sin_c * sin_f)
            sin = split(sin_c * cos_f + cos_c * sin_f)
            for part, table in ((0, high), (1, low)):
                table[turn, :freq_block, :rows_all] = cos[part]
                table[turn, :freq_block, rows_all:] = sin[part]
                table[turn, freq_block:, :rows_all] = -sin[part]
                table[turn, freq_block:, rows_all:] = cos[part]
            return carry

        def block(f, owner):
            return pix.at[f, rows_of(owner, row_block)]

        def up(f, hop):
            own = block(f, here.along(line - hop))
            return send(own, own, up_send.at[f, hop], up_recv.at[f, hop], here.along(1), here.me)

        def down(f, hop):
            own = block(f, here.along(hop))
            return send(own, own, down_send.at[f, hop], down_recv.at[f, hop], here.along(line - 1), here.me)

        def up_goes(hop):
            return (at >= hop) & (at < line - 1)

        def down_goes(hop):
            return (at < line - hop) & (at > 0)

        def enter(f):
            arrived(stage.at[f], in_recv.at[f])
            pix[f, rows_of(at, row_block)] = stage[f].T

            @pl.when(up_goes(0))
            def _():
                up(f, 0).start()

            @pl.when(down_goes(0))
            def _():
                down(f, 0).start()

        def relay(f, hop):
            @pl.when(at >= hop)
            def _():
                arrived(block(f, here.along(line - hop)), up_recv.at[f, hop - 1])

            if hop < line - 1:
                @pl.when(up_goes(hop))
                def _():
                    up(f, hop).start()

            @pl.when(at < line - hop)
            def _():
                arrived(block(f, here.along(hop)), down_recv.at[f, hop - 1])

            if hop < line - 1:
                @pl.when(down_goes(hop))
                def _():
                    down(f, hop).start()

        def leave(f, turn):
            k, j = f // pair, f % pair
            src = out.at[f % 2, turn]
            dst = spec.at[k, here.me * pair + j]
            if turn == 0:
                return pltpu.make_async_copy(src, dst, out_send.at[f, 0])
            return send(src, dst, out_send.at[f, turn], out_recv.at[f, turn], at, here.peers[turn])

        def sent(f):
            leave(f, 0).wait()
            for turn in range(1, 8):
                leave(f, turn).wait_send()

        def compute(f):
            half = product(split(pix[f]), (to_cols[0], to_cols[1]))
            for part in range(2):
                rows = slice(part * rows_all, (part + 1) * rows_all)
                half_high[rows, :], half_low[rows, :] = split(half[:, part * freq_width : (part + 1) * freq_width])

            @pl.when(f >= 2)
            def _():
                sent(f - 2)

            right = (half_high[...], half_low[...])
            for turn in TURNS:
                value = product((high[turn], low[turn]), right)
                out[f % 2, turn] = value.reshape(2, freq_block, freq_width)
                leave(f, turn).start()

        enter(0)
        lax.fori_loop(0, 8, build, 0)

        def step(f, carry):
            for hop in range(1, line - 1):
                relay(f, hop)

            @pl.when(f + 1 < fields)
            def _():
                enter(f + 1)

            relay(f, line - 1)
            compute(f)
            return carry

        lax.fori_loop(0, fields, step, 0)
        sent(fields - 2)
        sent(fields - 1)

        def finish(f, carry):
            for turn in range(1, 8):
                first(f, turn).wait_send()
                leave(f, turn).wait_recv()
            for hop in range(line - 1):
                @pl.when(up_goes(hop))
                def _():
                    up(f, hop).wait_send()

                @pl.when(down_goes(hop))
                def _():
                    down(f, hop).wait_send()
            return carry

        lax.fori_loop(0, fields, finish, 0)

    dma = pltpu.SemaphoreType.DMA
    vmem = pl.BlockSpec(memory_space=pltpu.VMEM)
    hbm = pl.BlockSpec(memory_space=pl.ANY)
    hops = dma((fields, line - 1))
    return pl.pallas_call(
        body,
        in_specs=[hbm, vmem, vmem, vmem],
        out_specs=hbm,
        out_shape=jax.ShapeDtypeStruct((rhs_count, seg_count, 2, freq_block, freq_width), jnp.float32),
        scratch_shapes=[
            pltpu.VMEM((fields, cols_all, row_block), jnp.float32),
            pltpu.VMEM((fields, rows_all, cols_all), jnp.float32),
            pltpu.VMEM((8, 2 * freq_block, 2 * rows_all), jnp.bfloat16),
            pltpu.VMEM((8, 2 * freq_block, 2 * rows_all), jnp.bfloat16),
            pltpu.VMEM((2 * rows_all, freq_width), jnp.bfloat16),
            pltpu.VMEM((2 * rows_all, freq_width), jnp.bfloat16),
            pltpu.VMEM((2, 8, 2, freq_block, freq_width), jnp.float32),
            dma((fields, 8)), dma((fields,)), hops, hops, hops, hops, dma((fields, 8)), dma((fields, 8)),
        ],
        compiler_params=pltpu.CompilerParams(
            collective_id=0, has_side_effects=True, vmem_limit_bytes=VMEM_LIMIT
        ),
        name="forward",
    )(packed, fine, coarse, to_cols)


def backward_call(mixed, scalars, fine, coarse, from_cols, line, row_block, col_block):
    rhs_count, seg_count, _, freq_block, freq_width = mixed.shape
    pair = seg_count // 8
    fields = rhs_count * pair
    rows_all, cols_all = row_block * line, col_block * 8

    def body(mixed, scalars, fine, coarse, from_cols, image, totals, got, part_sum, high, low,
             half_high, half_low, up_in, down_in, turned, line_sums, line_total, plane_sums,
             in_send, in_recv, up_send, up_recv, down_send, down_recv, out_send, out_recv,
             line_send, line_recv, plane_send, plane_recv):
        here = Place(line)
        at = here.at
        here.greet()

        def enter(f, turn):
            k, j = f // pair, f % pair
            src, dst = mixed.at[k, here.peers[turn] * pair + j], got.at[f, turn]
            if turn == 0:
                return pltpu.make_async_copy(src, dst, in_recv.at[f, 0])
            return send(src, dst, in_send.at[f, turn], in_recv.at[f, turn], at, here.peers[turn])

        def along_line(hops):
            return send(scalars, line_sums.at[hops], line_send.at[hops], line_recv.at[hops],
                        here.along(hops), here.me)

        def in_plane(turn):
            return send(line_total, plane_sums.at[turn], plane_send.at[turn], plane_recv.at[turn],
                        at, here.peers[turn])

        for hops in range(1, line):
            along_line(hops).start()

        def begin(f, carry):
            for turn in TURNS:
                enter(f, turn).start()
            return carry

        lax.fori_loop(0, fields, begin, 0)

        def build(turn, carry):
            cos_f, sin_f = fine[0], fine[1]
            cos_c, sin_c = coarse[0, turn], coarse[1, turn]
            cos = split(cos_c * cos_f - sin_c * sin_f)
            sin = split(sin_c * cos_f + cos_c * sin_f)
            for part, table in ((0, high), (1, low)):
                for half in range(2):
                    lanes = rows_of(turn * 2 + half, freq_block)
                    table[:rows_all, lanes] = -sin[part] if half else cos[part]
                    table[rows_all:, lanes] = cos[part] if half else sin[part]
            return carry

        lax.fori_loop(0, 8, build, 0)
        total = scalars[...]
        for hops in range(1, line):
            along_line(hops).wait()
            total = total + line_sums[hops]
        line_total[...] = total

        def block(f, owner):
            return part_sum.at[f, rows_of(owner, row_block)]

        def up(f, owner):
            return send(block(f, owner), up_in.at[f, owner - 1], up_send.at[f, owner - 1],
                        up_recv.at[f, owner - 1], here.along(1), here.me)

        def down(f, owner):
            return send(block(f, owner), down_in.at[f, owner], down_send.at[f, owner],
                        down_recv.at[f, owner], here.along(line - 1), here.me)

        def add(f, owner, extra):
            rows = rows_of(owner, row_block)
            part_sum[f, rows] = part_sum[f, rows] + extra

        def up_add(f, owner):
            arrived(up_in.at[f, owner - 1], up_recv.at[f, owner - 1])
            add(f, owner, up_in[f, owner - 1])

        def down_add(f, owner):
            arrived(down_in.at[f, owner], down_recv.at[f, owner])
            add(f, owner, down_in[f, owner])

        def compute(f):
            for turn in range(8):
                arrived(got.at[f, turn], in_recv.at[f, turn])
            spectrum = split(got[f].reshape(16 * freq_block, freq_width))
            half = product((high[...], low[...]), spectrum)
            for part in range(2):
                lanes = slice(part * freq_width, (part + 1) * freq_width)
                half_high[:, lanes], half_low[:, lanes] = split(half[part * rows_all : (part + 1) * rows_all])
            part_sum[f] = product((half_high[...], half_low[...]), (from_cols[0], from_cols[1]))

        def relay(f, hop):
            high_end, low_end = line - hop, hop - 1

            @pl.when((at > 0) & (at < high_end))
            def _():
                up_add(f, high_end)

            @pl.when(at < high_end)
            def _():
                up(f, high_end).start()

            @pl.when((at < line - 1) & (at > low_end))
            def _():
                down_add(f, low_end)

            @pl.when(at > low_end)
            def _():
                down(f, low_end).start()

        def leave(f, turn):
            k, j = f // pair, f % pair
            src = turned.at[f, rows_of(here.peers[turn], col_block)]
            dst = image.at[k, here.me * pair + j]
            if turn == 0:
                return pltpu.make_async_copy(src, dst, out_send.at[f, 0])
            return send(src, dst, out_send.at[f, turn], out_recv.at[f, turn], at, here.peers[turn])

        def final(f):
            @pl.when(at > 0)
            def _():
                up_add(f, at)

            @pl.when(at < line - 1)
            def _():
                down_add(f, at)

            turned[f] = part_sum[f, rows_of(at, row_block)].T
            for turn in TURNS:
                leave(f, turn).start()

        for turn in range(1, 8):
            in_plane(turn).start()

        def step(f, carry):
            @pl.when(f < fields)
            def _():
                compute(f)
                relay(f, 1)

            @pl.when(f > 0)
            def _():
                final(f - 1)

            @pl.when(f < fields)
            def _():
                for hop in range(2, line):
                    relay(f, hop)

            return carry

        lax.fori_loop(0, fields + 1, step, 0)
        total = line_total[...]
        for turn in range(1, 8):
            in_plane(turn).wait()
            total = total + plane_sums[turn]
        totals[...] = total

        def finish(f, carry):
            leave(f, 0).wait()
            for turn in range(1, 8):
                enter(f, turn).wait_send()
                leave(f, turn).wait()
            for owner in range(line):
                if owner > 0:
                    @pl.when(at < owner)
                    def _():
                        up(f, owner).wait_send()

                if owner < line - 1:
                    @pl.when(at > owner)
                    def _():
                        down(f, owner).wait_send()
            return carry

        lax.fori_loop(0, fields, finish, 0)

    dma = pltpu.SemaphoreType.DMA
    vmem = pl.BlockSpec(memory_space=pltpu.VMEM)
    hbm = pl.BlockSpec(memory_space=pl.ANY)
    hops = dma((fields, line - 1))
    stream = pltpu.VMEM((fields, line - 1, row_block, cols_all), jnp.float32)
    return pl.pallas_call(
        body,
        in_specs=[hbm, vmem, vmem, vmem, vmem],
        out_specs=[hbm, vmem],
        out_shape=[
            jax.ShapeDtypeStruct((rhs_count, seg_count, col_block, row_block), jnp.float32),
            jax.ShapeDtypeStruct(scalars.shape, jnp.float32),
        ],
        scratch_shapes=[
            pltpu.VMEM((fields, 8, 2, freq_block, freq_width), jnp.float32),
            pltpu.VMEM((fields, rows_all, cols_all), jnp.float32),
            pltpu.VMEM((2 * rows_all, 16 * freq_block), jnp.bfloat16),
            pltpu.VMEM((2 * rows_all, 16 * freq_block), jnp.bfloat16),
            pltpu.VMEM((rows_all, 2 * freq_width), jnp.bfloat16),
            pltpu.VMEM((rows_all, 2 * freq_width), jnp.bfloat16),
            stream, stream,
            pltpu.VMEM((fields, cols_all, row_block), jnp.float32),
            pltpu.VMEM((line,) + scalars.shape, jnp.float32),
            pltpu.VMEM(scalars.shape, jnp.float32),
            pltpu.VMEM((8,) + scalars.shape, jnp.float32),
            dma((fields, 8)), dma((fields, 8)), hops, hops, hops, hops, dma((fields, 8)), dma((fields, 8)),
            dma((line,)), dma((line,)), dma((8,)), dma((8,)),
        ],
        compiler_params=pltpu.CompilerParams(
            collective_id=1, has_side_effects=True, vmem_limit_bytes=VMEM_LIMIT
        ),
        name="backward",
    )(mixed, scalars, fine, coarse, from_cols)


def mix_all(symbol, spectra):
    freq_rows, freq_cols, pair_count = symbol.shape
    rhs_count, seg_count, parts = spectra.shape[:3]
    step = math.gcd(ROW_STEP, freq_rows)

    def body(symbol_ref, in_ref, out_ref, curve_ref, turned):
        def one(u, carry):
            turned[...] = symbol_ref[u].T
            sums = {}
            for t in range(seg_count):
                column = turned[t * seg_count : (t + 1) * seg_count, :]
                for part in range(parts):
                    for k in range(rhs_count):
                        term = column * in_ref[k, t, part, pl.ds(u, 1), :]
                        sums[part, k] = sums[part, k] + term if t else term
            for part in range(parts):
                for k in range(rhs_count):
                    for s in range(seg_count):
                        out_ref[k, s, part, pl.ds(u, 1), :] = sums[part, k][s : s + 1, :]
            return carry

        lax.fori_loop(0, step, one, 0)

        @pl.when(pl.program_id(0) == 0)
        def _():
            curve_ref[...] = jnp.zeros_like(curve_ref)

        for k in range(rhs_count):
            total = curve_ref[k]
            for t in range(seg_count):
                for part in range(parts):
                    total = total + in_ref[k, t, part] * out_ref[k, t, part]
            curve_ref[k] = total

    block = pl.BlockSpec((rhs_count, seg_count, parts, step, freq_cols), lambda i: (0, 0, 0, i, 0))
    return pl.pallas_call(
        body,
        grid=(freq_rows // step,),
        in_specs=[pl.BlockSpec((step, freq_cols, pair_count), lambda i: (i, 0, 0)), block],
        out_specs=[block, pl.BlockSpec((rhs_count, step, freq_cols), lambda i: (0, 0, 0))],
        out_shape=[
            jax.ShapeDtypeStruct(spectra.shape, jnp.float32),
            jax.ShapeDtypeStruct((rhs_count, step, freq_cols), jnp.float32),
        ],
        scratch_shapes=[pltpu.VMEM((pair_count, freq_cols), jnp.float32)],
        name="mix",
    )(symbol, spectra)


def halves(table):
    high = lax.reduce_precision(table, 8, 7)
    return jnp.stack([high, table - high]).astype(jnp.bfloat16)


def routed(right_side, symbol):
    line = lax.axis_size("row")
    rhs_count, seg_count, row_block, col_block = right_side.shape
    freq_block, freq_width = symbol.shape[:2]
    rows_all, cols_all = row_block * line, col_block * 8
    freq_rows, freq_cols = freq_block * 8, freq_width * line
    norm_factor = 1.0 / (freq_rows * freq_cols)
    owners = jnp.stack(Place(line).peers)
    fine = jnp.stack(tables(steps(freq_block)[:, None] * steps(rows_all)[None, :], freq_rows))
    coarse = jnp.stack(tables(owners[:, None] * steps(rows_all, freq_block)[None, :], freq_rows))
    to_cols = col_transform(freq_cols, cols_all, freq_width, lax.axis_index("row") * freq_width)
    norm_now = jnp.sum(right_side * right_side, axis=(1, 2, 3))
    spectra = forward_call(
        right_side.transpose(0, 1, 3, 2), fine, coarse,
        halves(to_cols.transpose(1, 0, 2).reshape(cols_all, 2 * freq_width)), line, freq_block, freq_width,
    )
    mixed, curve = mix_all(symbol, spectra)
    curve = jnp.sum(curve, axis=(1, 2)) * norm_factor
    scalars = jnp.broadcast_to(jnp.stack([norm_now, curve])[..., None], (2, rhs_count, 128))
    image, totals = backward_call(
        mixed, scalars, fine.transpose(0, 2, 1), coarse[..., None],
        halves(to_cols.transpose(0, 2, 1).reshape(2 * freq_width, cols_all)), line, row_block, col_block,
    )
    applied = image.transpose(0, 1, 3, 2) * norm_factor
    step_size = (totals[0, :, 0] / totals[1, :, 0])[:, None, None, None]
    return (step_size * right_side, right_side - step_size * applied)


def fits(mesh, right_side, symbol):
    ring, wide = mesh.shape["row"], mesh.shape["col"]
    _, seg_count, rows, cols = right_side.shape
    freq_rows, freq_cols = symbol.shape[:2]
    aligned = all(n % 128 == 0 for n in (rows // ring, freq_rows // wide, freq_cols // ring))
    return ring > 1 and wide == 8 and seg_count % 8 == 0 and cols // wide % 8 == 0 and aligned


def solution(mesh):
    placed = P(None, None, "row", "col")

    def whole(right_side, symbol):
        return jax.shard_map(
            routed if fits(mesh, right_side, symbol) else local,
            mesh=mesh,
            in_specs=(placed, P("col", "row", None)),
            out_specs=(placed, placed),
            check_vma=False,
        )(right_side, symbol)

    return whole
```

time: 430 us -> 316 us (0.73)
  Pallas kernels: 375 us -> 298 us
  blocking collectives: 38.2 us -> 0 us
    pallas_call x1, Pallas kernels: 176 us -> 128 us  [forward_call(): pl.pallas_call(body, in_specs=[hbm, vmem, vmem, vmem], out_specs=hbm, out...]
    psum x1 -> x0, blocking collectives: 38.2 us -> none  [routed(): norm_now, curve = lax.psum((norm_now, curve), ('row', 'col'))]
    pallas_call x1, Pallas kernels: 168 us -> 140 us  [backward_call(): pl.pallas_call(body, in_specs=[hbm, vmem, vmem, vmem, vmem], out_specs=[h...]
where the time goes in v1:
time: 316 us; the launch traced here: 315 us
  Pallas kernels  298 us (94%)
  other arithmetic  10.4 us (3%)
  local copies, waits for them, and re-layouts  6.4 us (2%)
    pallas_call x1, Pallas kernels, backward_call(): pl.pallas_call(body, in_specs=[hbm, vmem, vmem, vmem, vmem], out_specs=[h...  140 us
    pallas_call x1, Pallas kernels, forward_call(): pl.pallas_call(body, in_specs=[hbm, vmem, vmem, vmem], out_specs=hbm, out...  128 us
    pallas_call x1, Pallas kernels, mix_all(): pl.pallas_call(body, grid=(freq_rows // step,), in_specs=[pl.BlockSpec((s...  29.9 us

profile of v1, /device:TPU:0, one launch (start us, length us, event | category | flops | bytes accessed | tf_op | source)
XLA Modules:
  0.0 315.2 jit_solution(16571937015442405085)
XLA Ops:
  0.7 0.1 stack.75
  0.8 0.2 fusion.24
  0.9 0.6 fusion.27
  1.6 0.2 fusion.22
  1.9 0.2 fusion.20
  2.1 0.1 fusion.2
  2.2 0.8 copy.6
  3.0 0.8 reshape.130
  3.9 0.2 reduce-precision_convert_fusion.1
  4.1 1.1 pad_maximum_fusion.to_cols
  5.1 1.0 fusion.9
  6.2 0.9 fusion.28
  7.0 1.0 copy.7.fine
  8.0 127.7 %forward.1.in_ref = f32[2,16,2,128,256]{4,3,2,1,0:T(8,128)} custom-call(f32[2,16,64,128]{3,2,1,0:T(8,128)} %bitcast.40, f32[2,128,512]{2,1,0:T(8,128)} %copy.7.fine, f32[2,8,512]{2,1,0:T(8,128)} %get-tuple-element.35.coarse, bf16[2,512,512]{2,1,0:T(8,128)(2,1)} %pad_maximum_fusion.to_cols), custom_call_target="tpu_custom_call" | custom-call | tf_op jit(solution)/shard_map/forward/pallas_call | solution.py:356
  135.7 0.0 copy-start
  135.7 29.9 %mix.1 = (f32[2,16,2,128,256]{4,3,2,1,0:T(8,128)}, f32[2,8,256]{2,1,0:T(8,128)}) custom-call(f32[128,256,256]{2,1,0:T(8,128)} %symbol_ref.1, f32[2,16,2,128,256]{4,3,2,1,0:T(8,128)} %forward.1.in_ref), custom_call_target="tpu_custom_call" | custom-call | tf_op jit(solution)/shard_map/mix/pallas_call | solution.py:625
  165.6 0.8 reduce_sum.19
  166.5 0.0 copy-done
  166.5 0.2 multiply_reduce_fusion
  166.7 0.7 broadcast_in_dim.4.scalars
  167.4 2.6 copy.9.coarse
  170.0 0.3 copy.8
  170.3 0.2 reduce-precision_convert_fusion
  170.5 1.1 pad_maximum_fusion.1.from_cols
  171.5 140.0 %backward.1 = (f32[2,16,64,128]{3,2,1,0:T(8,128)}, f32[2,2,128]{2,1,0:T(2,128)}) custom-call(f32[2,16,2,128,256]{4,3,2,1,0:T(8,128)} %get-tuple-element.22.mixed, f32[2,2,128]{2,1,0:T(2,128)} %broadcast_in_dim.4.scalars, f32[2,512,128]{2,1,0:T(8,128)} %get-tuple-element.32.fine, f32[2,8,512,1]{3,2,1,0:T(8,128)} %copy.9.coarse, ...), custom_call_target="tpu_custom_call" | custom-call | tf_op jit(solution)/shard_map/backward/pallas_call | solution.py:560
  311.6 0.8 fusion.26
  312.3 2.9 bitcast_subtract_fusion
  (10 shorter events, 0.1 us)
Async XLA Ops:
  135.7 30.8 %copy-start = (f32[2,16,128,64]{2,3,1,0:T(8,128)S(1)}, f32[2,16,128,64]{2,3,1,0:T(8,128)}, u32[]{:S(2)}) copy-start(f32[2,16,128,64]{2,3,1,0:T(8,128)} %param.2) | copy-start | bytes 3145732

commit v2 on v1

--- a/solution.py
+++ b/solution.py
@@ -160,6 +160,83 @@
     return one(left[0], right[0]) + (one(left[1], right[0]) + one(left[0], right[1]))
 
 
+def product_across(left, right):
+    def one(a, b):
+        return lax.dot_general(a, b, (((1,), (1,)), ((), ())), preferred_element_type=jnp.float32)
+
+    return one(left[0], right[0]) + (one(left[1], right[0]) + one(left[0], right[1]))
+
+
+def mix_scratch(symbol, seg_count, step):
+    freq_rows, freq_cols, pair_count = symbol.shape
+    block = pltpu.VMEM((2, seg_count, 2, step, freq_cols), jnp.float32)
+    dma = pltpu.SemaphoreType.DMA
+    return [
+        pltpu.VMEM((2, step, freq_cols, pair_count), jnp.float32), block, block,
+        pltpu.VMEM((pair_count, freq_cols), jnp.float32),
+        dma((2,)), dma((2,)), dma((2,)),
+    ]
+
+
+def mix_one(symbol, spectra, mixed, curve, scratch):
+    symbols, ins, outs, turned, symbol_sem, in_sem, out_sem = scratch
+    seg_count, parts, freq_rows, _ = spectra.shape
+    step = symbols.shape[1]
+    count = freq_rows // step
+
+    def load(c):
+        rows, slot = rows_of(c, step), c % 2
+        pltpu.make_async_copy(symbol.at[rows], symbols.at[slot], symbol_sem.at[slot]).start()
+        pltpu.make_async_copy(spectra.at[:, :, rows], ins.at[slot], in_sem.at[slot]).start()
+
+    def store(c):
+        slot = c % 2
+        return pltpu.make_async_copy(outs.at[slot], mixed.at[:, :, rows_of(c, step)], out_sem.at[slot])
+
+    load(0)
+    curve[...] = jnp.zeros_like(curve)
+
+    def chunk(c, carry):
+        slot = c % 2
+
+        @pl.when(c + 1 < count)
+        def _():
+            load(c + 1)
+
+        arrived(symbols.at[slot], symbol_sem.at[slot])
+        arrived(ins.at[slot], in_sem.at[slot])
+
+        @pl.when(c >= 2)
+        def _():
+            store(c - 2).wait()
+
+        def one(u, inner):
+            turned[...] = symbols[slot, u].T
+            sums = [None] * parts
+            for t in range(seg_count):
+                column = turned[t * seg_count : (t + 1) * seg_count, :]
+                for part in range(parts):
+                    term = column * ins[slot, t, part, pl.ds(u, 1), :]
+                    sums[part] = sums[part] + term if t else term
+            for part in range(parts):
+                for t in range(seg_count):
+                    outs[slot, t, part, pl.ds(u, 1), :] = sums[part][t : t + 1, :]
+            return inner
+
+        lax.fori_loop(0, step, one, 0)
+        total = curve[...]
+        for t in range(seg_count):
+            for part in range(parts):
+                total = total + ins[slot, t, part] * outs[slot, t, part]
+        curve[...] = total
+        store(c).start()
+        return carry
+
+    lax.fori_loop(0, count, chunk, 0)
+    store(count - 2).wait()
+    store(count - 1).wait()
+
+
 class Place:
     def __init__(self, line):
         self.line = line
@@ -201,14 +278,16 @@
 TURNS = (6, 2, 4, 7, 3, 5, 1, 0)
 
 
-def forward_call(packed, fine, coarse, to_cols, line, freq_block, freq_width):
+def forward_call(packed, symbol, fine, coarse, to_cols, line):
+    freq_block, freq_width = symbol.shape[:2]
+    mix_step = math.gcd(ROW_STEP, freq_block)
     rhs_count, seg_count, col_block, row_block = packed.shape
     pair = seg_count // 8
     fields = rhs_count * pair
     rows_all, cols_all = row_block * line, col_block * 8
 
-    def body(packed, fine, coarse, to_cols, spec, stage, pix, high, low, half_high, half_low, out,
-             in_send, in_recv, up_send, up_recv, down_send, down_recv, out_send, out_recv):
+    def body(packed, symbol, fine, coarse, to_cols, spec, mixed, curve, stage, pix, high, low, half_high, half_low, out,
+             in_send, in_recv, up_send, up_recv, down_send, down_recv, out_send, out_recv, *mix_refs):
         here = Place(line)
         at = here.at
         here.greet()
@@ -330,13 +409,21 @@
             return carry
 
         lax.fori_loop(0, fields, step, 0)
+
+        def landed(f, carry):
+            for turn in range(1, 8):
+                leave(f, turn).wait_recv()
+            return carry
+
+        lax.fori_loop(0, pair, landed, 0)
+        mix_one(symbol, spec.at[0], mixed, curve, mix_refs)
+        lax.fori_loop(pair, fields, landed, 0)
         sent(fields - 2)
         sent(fields - 1)
 
         def finish(f, carry):
             for turn in range(1, 8):
                 first(f, turn).wait_send()
-                leave(f, turn).wait_recv()
             for hop in range(line - 1):
                 @pl.when(up_goes(hop))
                 def _():
@@ -355,9 +442,13 @@
     hops = dma((fields, line - 1))
     return pl.pallas_call(
         body,
-        in_specs=[hbm, vmem, vmem, vmem],
-        out_specs=hbm,
-        out_shape=jax.ShapeDtypeStruct((rhs_count, seg_count, 2, freq_block, freq_width), jnp.float32),
+        in_specs=[hbm, hbm, vmem, vmem, vmem],
+        out_specs=[hbm, hbm, vmem],
+        out_shape=[
+            jax.ShapeDtypeStruct((rhs_count, seg_count, 2, freq_block, freq_width), jnp.float32),
+            jax.ShapeDtypeStruct((seg_count, 2, freq_block, freq_width), jnp.float32),
+            jax.ShapeDtypeStruct((mix_step, freq_width), jnp.float32),
+        ],
         scratch_shapes=[
             pltpu.VMEM((fields, cols_all, row_block), jnp.float32),
             pltpu.VMEM((fields, rows_all, cols_all), jnp.float32),
@@ -367,31 +458,35 @@
             pltpu.VMEM((2 * rows_all, freq_width), jnp.bfloat16),
             pltpu.VMEM((2, 8, 2, freq_block, freq_width), jnp.float32),
             dma((fields, 8)), dma((fields,)), hops, hops, hops, hops, dma((fields, 8)), dma((fields, 8)),
-        ],
+        ] + mix_scratch(symbol, seg_count, mix_step),
         compiler_params=pltpu.CompilerParams(
             collective_id=0, has_side_effects=True, vmem_limit_bytes=VMEM_LIMIT
         ),
         name="forward",
-    )(packed, fine, coarse, to_cols)
-
-
-def backward_call(mixed, scalars, fine, coarse, from_cols, line, row_block, col_block):
-    rhs_count, seg_count, _, freq_block, freq_width = mixed.shape
+    )(packed, symbol, fine, coarse, to_cols)
+
+
+def backward_call(symbol, spectra, mixed, norms, curve, fine, coarse, to_cols, line, row_block, col_block):
+    rhs_count, seg_count, _, freq_block, freq_width = spectra.shape
+    mix_step = curve.shape[0]
+    sums_shape = (2,) + norms.shape
     pair = seg_count // 8
     fields = rhs_count * pair
     rows_all, cols_all = row_block * line, col_block * 8
 
-    def body(mixed, scalars, fine, coarse, from_cols, image, totals, got, part_sum, high, low,
-             half_high, half_low, up_in, down_in, turned, line_sums, line_total, plane_sums,
+    def body(symbol, spectra, mixed, norms, curve, fine, coarse, to_cols, image, totals, mixed_last,
+             got, part_sum, high, low,
+             half_high, half_low, up_in, down_in, turned, scalars, line_sums, line_total, plane_sums, curve_last,
              in_send, in_recv, up_send, up_recv, down_send, down_recv, out_send, out_recv,
-             line_send, line_recv, plane_send, plane_recv):
+             line_send, line_recv, plane_send, plane_recv, *mix_refs):
         here = Place(line)
         at = here.at
         here.greet()
 
-        def enter(f, turn):
-            k, j = f // pair, f % pair
-            src, dst = mixed.at[k, here.peers[turn] * pair + j], got.at[f, turn]
+        def enter(last, j, turn):
+            f = last * pair + j
+            src = (mixed_last if last else mixed).at[here.peers[turn] * pair + j]
+            dst = got.at[f, turn]
             if turn == 0:
                 return pltpu.make_async_copy(src, dst, in_recv.at[f, 0])
             return send(src, dst, in_send.at[f, turn], in_recv.at[f, turn], at, here.peers[turn])
@@ -404,21 +499,18 @@
             return send(line_total, plane_sums.at[turn], plane_send.at[turn], plane_recv.at[turn],
                         at, here.peers[turn])
 
-        for hops in range(1, line):
-            along_line(hops).start()
-
-        def begin(f, carry):
-            for turn in TURNS:
-                enter(f, turn).start()
-            return carry
-
-        lax.fori_loop(0, fields, begin, 0)
+        def begin(last):
+            for j in range(pair):
+                for turn in TURNS:
+                    enter(last, j, turn).start()
+
+        begin(0)
 
         def build(turn, carry):
+            cos_c, sin_c = coarse[0, pl.ds(turn, 1), :], coarse[1, pl.ds(turn, 1), :]
             cos_f, sin_f = fine[0], fine[1]
-            cos_c, sin_c = coarse[0, turn], coarse[1, turn]
-            cos = split(cos_c * cos_f - sin_c * sin_f)
-            sin = split(sin_c * cos_f + cos_c * sin_f)
+            cos = split((cos_c * cos_f - sin_c * sin_f).T)
+            sin = split((sin_c * cos_f + cos_c * sin_f).T)
             for part, table in ((0, high), (1, low)):
                 for half in range(2):
                     lanes = rows_of(turn * 2 + half, freq_block)
@@ -426,7 +518,15 @@
                     table[rows_all:, lanes] = cos[part] if half else sin[part]
             return carry
 
+        mix_one(symbol, spectra.at[rhs_count - 1], mixed_last, curve_last, mix_refs)
+        begin(1)
+        scalars[0] = norms[...]
+        for k, part in ((0, curve), (1, curve_last)):
+            whole = jnp.sum(jnp.sum(part[...], axis=0, keepdims=True), axis=1, keepdims=True)
+            scalars[1, k : k + 1, :] = jnp.broadcast_to(whole, (1, norms.shape[1]))
         lax.fori_loop(0, 8, build, 0)
+        for hops in range(1, line):
+            along_line(hops).start()
         total = scalars[...]
         for hops in range(1, line):
             along_line(hops).wait()
@@ -464,7 +564,7 @@
             for part in range(2):
                 lanes = slice(part * freq_width, (part + 1) * freq_width)
                 half_high[:, lanes], half_low[:, lanes] = split(half[part * rows_all : (part + 1) * rows_all])
-            part_sum[f] = product((half_high[...], half_low[...]), (from_cols[0], from_cols[1]))
+            part_sum[f] = product_across((half_high[...], half_low[...]), (to_cols[0], to_cols[1]))
 
         def relay(f, hop):
             high_end, low_end = line - hop, hop - 1
@@ -536,7 +636,6 @@
         def finish(f, carry):
             leave(f, 0).wait()
             for turn in range(1, 8):
-                enter(f, turn).wait_send()
                 leave(f, turn).wait()
             for owner in range(line):
                 if owner > 0:
@@ -551,6 +650,10 @@
             return carry
 
         lax.fori_loop(0, fields, finish, 0)
+        for last in range(2):
+            for j in range(pair):
+                for turn in range(1, 8):
+                    enter(last, j, turn).wait_send()
 
     dma = pltpu.SemaphoreType.DMA
     vmem = pl.BlockSpec(memory_space=pltpu.VMEM)
@@ -559,11 +662,12 @@
     stream = pltpu.VMEM((fields, line - 1, row_block, cols_all), jnp.float32)
     return pl.pallas_call(
         body,
-        in_specs=[hbm, vmem, vmem, vmem, vmem],
-        out_specs=[hbm, vmem],
+        in_specs=[hbm, hbm, hbm, vmem, vmem, vmem, vmem, vmem],
+        out_specs=[hbm, vmem, hbm],
         out_shape=[
             jax.ShapeDtypeStruct((rhs_count, seg_count, col_block, row_block), jnp.float32),
-            jax.ShapeDtypeStruct(scalars.shape, jnp.float32),
+            jax.ShapeDtypeStruct(sums_shape, jnp.float32),
+            jax.ShapeDtypeStruct(mixed.shape, jnp.float32),
         ],
         scratch_shapes=[
             pltpu.VMEM((fields, 8, 2, freq_block, freq_width), jnp.float32),
@@ -574,66 +678,19 @@
             pltpu.VMEM((rows_all, 2 * freq_width), jnp.bfloat16),
             stream, stream,
             pltpu.VMEM((fields, cols_all, row_block), jnp.float32),
-            pltpu.VMEM((line,) + scalars.shape, jnp.float32),
-            pltpu.VMEM(scalars.shape, jnp.float32),
-            pltpu.VMEM((8,) + scalars.shape, jnp.float32),
+            pltpu.VMEM(sums_shape, jnp.float32),
+            pltpu.VMEM((line,) + sums_shape, jnp.float32),
+            pltpu.VMEM(sums_shape, jnp.float32),
+            pltpu.VMEM((8,) + sums_shape, jnp.float32),
+            pltpu.VMEM(curve.shape, jnp.float32),
             dma((fields, 8)), dma((fields, 8)), hops, hops, hops, hops, dma((fields, 8)), dma((fields, 8)),
             dma((line,)), dma((line,)), dma((8,)), dma((8,)),
-        ],
+        ] + mix_scratch(symbol, seg_count, mix_step),
         compiler_params=pltpu.CompilerParams(
             collective_id=1, has_side_effects=True, vmem_limit_bytes=VMEM_LIMIT
         ),
         name="backward",
-    )(mixed, scalars, fine, coarse, from_cols)
-
-
-def mix_all(symbol, spectra):
-    freq_rows, freq_cols, pair_count = symbol.shape
-    rhs_count, seg_count, parts = spectra.shape[:3]
-    step = math.gcd(ROW_STEP, freq_rows)
-
-    def body(symbol_ref, in_ref, out_ref, curve_ref, turned):
-        def one(u, carry):
-            turned[...] = symbol_ref[u].T
-            sums = {}
-            for t in range(seg_count):
-                column = turned[t * seg_count : (t + 1) * seg_count, :]
-                for part in range(parts):
-                    for k in range(rhs_count):
-                        term = column * in_ref[k, t, part, pl.ds(u, 1), :]
-                        sums[part, k] = sums[part, k] + term if t else term
-            for part in range(parts):
-                for k in range(rhs_count):
-                    for s in range(seg_count):
-                        out_ref[k, s, part, pl.ds(u, 1), :] = sums[part, k][s : s + 1, :]
-            return carry
-
-        lax.fori_loop(0, step, one, 0)
-
-        @pl.when(pl.program_id(0) == 0)
-        def _():
-            curve_ref[...] = jnp.zeros_like(curve_ref)
-
-        for k in range(rhs_count):
-            total = curve_ref[k]
-            for t in range(seg_count):
-                for part in range(parts):
-                    total = total + in_ref[k, t, part] * out_ref[k, t, part]
-            curve_ref[k] = total
-
-    block = pl.BlockSpec((rhs_count, seg_count, parts, step, freq_cols), lambda i: (0, 0, 0, i, 0))
-    return pl.pallas_call(
-        body,
-        grid=(freq_rows // step,),
-        in_specs=[pl.BlockSpec((step, freq_cols, pair_count), lambda i: (i, 0, 0)), block],
-        out_specs=[block, pl.BlockSpec((rhs_count, step, freq_cols), lambda i: (0, 0, 0))],
-        out_shape=[
-            jax.ShapeDtypeStruct(spectra.shape, jnp.float32),
-            jax.ShapeDtypeStruct((rhs_count, step, freq_cols), jnp.float32),
-        ],
-        scratch_shapes=[pltpu.VMEM((pair_count, freq_cols), jnp.float32)],
-        name="mix",
-    )(symbol, spectra)
+    )(symbol, spectra, mixed, norms, curve, fine, coarse, to_cols)
 
 
 def halves(table):
@@ -653,28 +710,23 @@
     coarse = jnp.stack(tables(owners[:, None] * steps(rows_all, freq_block)[None, :], freq_rows))
     to_cols = col_transform(freq_cols, cols_all, freq_width, lax.axis_index("row") * freq_width)
     norm_now = jnp.sum(right_side * right_side, axis=(1, 2, 3))
-    spectra = forward_call(
-        right_side.transpose(0, 1, 3, 2), fine, coarse,
-        halves(to_cols.transpose(1, 0, 2).reshape(cols_all, 2 * freq_width)), line, freq_block, freq_width,
-    )
-    mixed, curve = mix_all(symbol, spectra)
-    curve = jnp.sum(curve, axis=(1, 2)) * norm_factor
-    scalars = jnp.broadcast_to(jnp.stack([norm_now, curve])[..., None], (2, rhs_count, 128))
-    image, totals = backward_call(
-        mixed, scalars, fine.transpose(0, 2, 1), coarse[..., None],
-        halves(to_cols.transpose(0, 2, 1).reshape(2 * freq_width, cols_all)), line, row_block, col_block,
+    norms = jnp.broadcast_to(norm_now[:, None], (rhs_count, 128))
+    to_cols = halves(to_cols.transpose(1, 0, 2).reshape(cols_all, 2 * freq_width))
+    spectra, mixed, curve = forward_call(right_side.transpose(0, 1, 3, 2), symbol, fine, coarse, to_cols, line)
+    image, totals, _ = backward_call(
+        symbol, spectra, mixed, norms, curve, fine, coarse, to_cols, line, row_block, col_block
     )
     applied = image.transpose(0, 1, 3, 2) * norm_factor
-    step_size = (totals[0, :, 0] / totals[1, :, 0])[:, None, None, None]
+    step_size = (totals[0, :, 0] / (totals[1, :, 0] * norm_factor))[:, None, None, None]
     return (step_size * right_side, right_side - step_size * applied)
 
 
 def fits(mesh, right_side, symbol):
     ring, wide = mesh.shape["row"], mesh.shape["col"]
-    _, seg_count, rows, cols = right_side.shape
+    rhs_count, seg_count, rows, cols = right_side.shape
     freq_rows, freq_cols = symbol.shape[:2]
     aligned = all(n % 128 == 0 for n in (rows // ring, freq_rows // wide, freq_cols // ring))
-    return ring > 1 and wide == 8 and seg_count % 8 == 0 and cols // wide % 8 == 0 and aligned
+    return ring > 1 and wide == 8 and rhs_count == 2 and seg_count % 8 == 0 and cols // wide % 8 == 0 and aligned
 
 
 def solution(mesh):

time: 316 us -> 281 us (0.89)
  Pallas kernels: 298 us -> 267 us
  local copies, waits for them, and re-layouts: 6.4 us -> 1.66 us
    pallas_call x3 -> x2, Pallas kernels: 298 us -> 267 us  [the longest x1 139 us: backward_call(): pl.pallas_call(body, in_specs=[hbm, hbm, hbm, vmem, vmem, vmem, vmem, vme...]
where the time goes in v2:
time: 281 us; the launch traced here: 280 us
  Pallas kernels  267 us (95%)
  other arithmetic  10.5 us (4%)
    pallas_call x1, Pallas kernels, backward_call(): pl.pallas_call(body, in_specs=[hbm, hbm, hbm, vmem, vmem, vmem, vmem, vme...  139 us
    pallas_call x1, Pallas kernels, forward_call(): pl.pallas_call(body, in_specs=[hbm, hbm, vmem, vmem, vmem], out_specs=[hb...  128 us

profile of v2, /device:TPU:0, one launch (start us, length us, event | category | flops | bytes accessed | tf_op | source)
XLA Modules:
  0.0 279.8 jit_solution(11736758685400629902)
XLA Ops:
  0.7 0.1 stack.62
  0.8 1.5 multiply_reduce_fusion
  2.2 0.6 broadcast_in_dim.2.norms
  2.9 0.2 fusion.23
  3.1 0.6 pad_maximum_fusion.2.coarse
  3.7 0.6 fusion.21
  4.3 0.2 fusion.19
  4.6 0.6 fusion.1
  5.2 0.8 reshape.98
  6.0 0.2 reduce-precision_convert_fusion
  6.2 1.1 pad_maximum_fusion.to_cols
  7.3 1.0 fusion.8
  8.3 0.8 pad_maximum_fusion.1.fine
  9.1 128.3 %forward.1 = (f32[2,16,2,128,256]{4,3,2,1,0:T(8,128)}, f32[16,2,128,256]{3,2,1,0:T(8,128)}, f32[8,256]{1,0:T(8,128)}) custom-call(f32[2,16,64,128]{3,2,1,0:T(8,128)} %bitcast.26, f32[128,256,256]{2,1,0:T(8,128)} %symbol.3, f32[2,128,512]{2,1,0:T(8,128)} %pad_maximum_fusion.1.fine, f32[2,8,512]{2,1,0:T(8,128)} %pad_maximum_fusion.2.coarse, ...), custom_call_target="tpu_custom_call" | custom-call | tf_op jit(solution)/shard_map/forward/pallas_call | solution.py:443
  137.4 0.0 copy-start
  137.5 138.5 %backward.1 = (f32[2,16,64,128]{3,2,1,0:T(8,128)}, f32[2,2,128]{2,1,0:T(2,128)}, f32[16,2,128,256]{3,2,1,0:T(8,128)}) custom-call(f32[128,256,256]{2,1,0:T(8,128)} %symbol.3, f32[2,16,2,128,256]{4,3,2,1,0:T(8,128)} %get-tuple-element.23.spectra, f32[16,2,128,256]{3,2,1,0:T(8,128)} %get-tuple-element.24.mixed, f32[2,128]{1,0:T(2,128)} %broadcast_in_dim.2.norms, ...), custom_call_target="tpu_custom_call" | custom-call | tf_op jit(solution)/shard_map/backward/pallas_call | solution.py:663
  276.0 0.8 fusion.25
  276.8 0.0 copy-done
  276.8 3.0 %bitcast_subtract_fusion = (f32[2,16,128,64]{2,3,1,0:T(8,128)}, f32[2,16,128,64]{2,3,1,0:T(8,128)}) fusion(f32[2,16,128,64]{2,3,1,0:T(8,128)S(1)} %copy-done, f32[2,16,64,128]{3,2,1,0:T(8,128)} %get-tuple-element.27, f32[2]{0:T(128)S(1)} %broadcast_multiply_fusion.1, f32[2]{0:T(128)S(1)} %fusion.25), kind=kLoop, calls=%fused_computation.4 | loop fusion | flops 786432 | bytes 4194320 | tf_op jit(solution)/shard_map/sub | solution.py:721
  (8 shorter events, 0.1 us)
Async XLA Ops:
  137.4 139.3 %copy-start = (f32[2,16,128,64]{2,3,1,0:T(8,128)S(1)}, f32[2,16,128,64]{2,3,1,0:T(8,128)}, u32[]{:S(2)}) copy-start(f32[2,16,128,64]{2,3,1,0:T(8,128)} %param.2) | copy-start | bytes 3145732

commit v3 on v2

--- a/solution.py
+++ b/solution.py
@@ -278,7 +278,190 @@
 TURNS = (6, 2, 4, 7, 3, 5, 1, 0)
 
 
-def forward_call(packed, symbol, fine, coarse, to_cols, line):
+def backward_parts(here, sizes, operands, scratch):
+    pair, fields, rows_all, row_block, col_block, freq_block, freq_width = sizes
+    norms, fine, coarse, to_cols, mixed, mixed_last, curve, curve_last, image, totals = operands
+    (got, part_sum, high, low, half_high, half_low, up_in, down_in, turned,
+     scalars, line_sums, line_total, plane_sums,
+     in_send, in_recv, up_send, up_recv, down_send, down_recv, out_send, out_recv,
+     line_send, line_recv, plane_send, plane_recv) = scratch
+    line, at = here.line, here.at
+
+    def enter(last, j, turn):
+        f = last * pair + j
+        src = (mixed_last if last else mixed).at[here.peers[turn] * pair + j]
+        dst = got.at[f, turn]
+        if turn == 0:
+            return pltpu.make_async_copy(src, dst, in_recv.at[f, 0])
+        return send(src, dst, in_send.at[f, turn], in_recv.at[f, turn], at, here.peers[turn])
+
+    def along_line(hops):
+        return send(scalars, line_sums.at[hops], line_send.at[hops], line_recv.at[hops],
+                    here.along(hops), here.me)
+
+    def in_plane(turn):
+        return send(line_total, plane_sums.at[turn], plane_send.at[turn], plane_recv.at[turn],
+                    at, here.peers[turn])
+
+    def begin(last):
+        for j in range(pair):
+            for turn in TURNS:
+                enter(last, j, turn).start()
+
+    def build(turn, carry):
+        cos_c, sin_c = coarse[0, pl.ds(turn, 1), :], coarse[1, pl.ds(turn, 1), :]
+        cos_f, sin_f = fine[0], fine[1]
+        cos = split((cos_c * cos_f - sin_c * sin_f).T)
+        sin = split((sin_c * cos_f + cos_c * sin_f).T)
+        for part, table in ((0, high), (1, low)):
+            for half in range(2):
+                lanes = rows_of(turn * 2 + half, freq_block)
+                table[:rows_all, lanes] = -sin[part] if half else cos[part]
+                table[rows_all:, lanes] = cos[part] if half else sin[part]
+        return carry
+
+    def share():
+        scalars[0] = norms[...]
+        for k, part in ((0, curve), (1, curve_last)):
+            whole = jnp.sum(jnp.sum(part[...], axis=0, keepdims=True), axis=1, keepdims=True)
+            scalars[1, k : k + 1, :] = jnp.broadcast_to(whole, (1, norms.shape[1]))
+        for hops in range(1, line):
+            along_line(hops).start()
+
+    def share_plane():
+        total = scalars[...]
+        for hops in range(1, line):
+            along_line(hops).wait()
+            total = total + line_sums[hops]
+        line_total[...] = total
+        for turn in range(1, 8):
+            in_plane(turn).start()
+
+    def block(f, owner):
+        return part_sum.at[f, rows_of(owner, row_block)]
+
+    def up(f, owner):
+        return send(block(f, owner), up_in.at[f, owner - 1], up_send.at[f, owner - 1],
+                    up_recv.at[f, owner - 1], here.along(1), here.me)
+
+    def down(f, owner):
+        return send(block(f, owner), down_in.at[f, owner], down_send.at[f, owner],
+                    down_recv.at[f, owner], here.along(line - 1), here.me)
+
+    def add(f, owner, extra):
+        rows = rows_of(owner, row_block)
+        part_sum[f, rows] = part_sum[f, rows] + extra
+
+    def up_add(f, owner):
+        arrived(up_in.at[f, owner - 1], up_recv.at[f, owner - 1])
+        add(f, owner, up_in[f, owner - 1])
+
+    def down_add(f, owner):
+        arrived(down_in.at[f, owner], down_recv.at[f, owner])
+        add(f, owner, down_in[f, owner])
+
+    def compute(f):
+        for turn in range(8):
+            arrived(got.at[f, turn], in_recv.at[f, turn])
+        spectrum = split(got[f].reshape(16 * freq_block, freq_width))
+        half = product((high[...], low[...]), spectrum)
+        for part in range(2):
+            lanes = slice(part * freq_width, (part + 1) * freq_width)
+            half_high[:, lanes], half_low[:, lanes] = split(half[part * rows_all : (part + 1) * rows_all])
+        part_sum[f] = product_across((half_high[...], half_low[...]), (to_cols[0], to_cols[1]))
+
+    def relay(f, hop):
+        high_end, low_end = line - hop, hop - 1
+
+        @pl.when((at > 0) & (at < high_end))
+        def _():
+            up_add(f, high_end)
+
+        @pl.when(at < high_end)
+        def _():
+            up(f, high_end).start()
+
+        @pl.when((at < line - 1) & (at > low_end))
+        def _():
+            down_add(f, low_end)
+
+        @pl.when(at > low_end)
+        def _():
+            down(f, low_end).start()
+
+    def leave(f, turn):
+        k, j = f // pair, f % pair
+        src = turned.at[f, rows_of(here.peers[turn], col_block)]
+        dst = image.at[k, here.me * pair + j]
+        if turn == 0:
+            return pltpu.make_async_copy(src, dst, out_send.at[f, 0])
+        return send(src, dst, out_send.at[f, turn], out_recv.at[f, turn], at, here.peers[turn])
+
+    def final(f):
+        @pl.when(at > 0)
+        def _():
+            up_add(f, at)
+
+        @pl.when(at < line - 1)
+        def _():
+            down_add(f, at)
+
+        turned[f] = part_sum[f, rows_of(at, row_block)].T
+        for turn in TURNS:
+            leave(f, turn).start()
+
+    def step(f, carry):
+        @pl.when(f < fields)
+        def _():
+            compute(f)
+            relay(f, 1)
+
+        @pl.when(f > 0)
+        def _():
+            final(f - 1)
+
+        @pl.when(f < fields)
+        def _():
+            for hop in range(2, line):
+                relay(f, hop)
+
+        return carry
+
+    def run():
+        lax.fori_loop(0, fields + 1, step, 0)
+        total = line_total[...]
+        for turn in range(1, 8):
+            in_plane(turn).wait()
+            total = total + plane_sums[turn]
+        totals[...] = total
+
+    def finish(f, carry):
+        leave(f, 0).wait()
+        for turn in range(1, 8):
+            leave(f, turn).wait()
+        for owner in range(line):
+            if owner > 0:
+                @pl.when(at < owner)
+                def _():
+                    up(f, owner).wait_send()
+
+            if owner < line - 1:
+                @pl.when(at > owner)
+                def _():
+                    down(f, owner).wait_send()
+        return carry
+
+    def done():
+        lax.fori_loop(0, fields, finish, 0)
+        for last in range(2):
+            for j in range(pair):
+                for turn in range(1, 8):
+                    enter(last, j, turn).wait_send()
+
+    return begin, lambda: lax.fori_loop(0, 8, build, 0), share, share_plane, run, done
+
+
+def operate_call(packed, symbol, norms, fine, coarse, to_cols, line):
     freq_block, freq_width = symbol.shape[:2]
     mix_step = math.gcd(ROW_STEP, freq_block)
     rhs_count, seg_count, col_block, row_block = packed.shape
@@ -286,11 +469,17 @@
     fields = rhs_count * pair
     rows_all, cols_all = row_block * line, col_block * 8
 
-    def body(packed, symbol, fine, coarse, to_cols, spec, mixed, curve, stage, pix, high, low, half_high, half_low, out,
-             in_send, in_recv, up_send, up_recv, down_send, down_recv, out_send, out_recv, *mix_refs):
+    def body(packed, symbol, norms, fine, coarse, to_cols, image, totals, spec, mixed, mixed_last, *scratch):
+        (stage, pix, high, low, half_high, half_low, out, curve, curve_last,
+         in_send, in_recv, up_send, up_recv, down_send, down_recv, out_send, out_recv) = scratch[:17]
+        mix_refs, back_refs = scratch[17:24], scratch[24:]
         here = Place(line)
         at = here.at
         here.greet()
+        begin, build_back, share, share_plane, run, done = backward_parts(
+            here, (pair, fields, rows_all, row_block, col_block, freq_block, freq_width),
+            (norms, fine, coarse, to_cols, mixed, mixed_last, curve, curve_last, image, totals), back_refs,
+        )
 
         def first(f, turn):
             k, j = f // pair, f % pair
@@ -417,9 +606,16 @@
 
         lax.fori_loop(0, pair, landed, 0)
         mix_one(symbol, spec.at[0], mixed, curve, mix_refs)
+        begin(0)
+        build_back()
         lax.fori_loop(pair, fields, landed, 0)
         sent(fields - 2)
         sent(fields - 1)
+        mix_one(symbol, spec.at[1], mixed_last, curve_last, mix_refs)
+        begin(1)
+        share()
+        share_plane()
+        run()
 
         def finish(f, carry):
             for turn in range(1, 8):
@@ -435,262 +631,54 @@
             return carry
 
         lax.fori_loop(0, fields, finish, 0)
-
-    dma = pltpu.SemaphoreType.DMA
-    vmem = pl.BlockSpec(memory_space=pltpu.VMEM)
-    hbm = pl.BlockSpec(memory_space=pl.ANY)
-    hops = dma((fields, line - 1))
-    return pl.pallas_call(
-        body,
-        in_specs=[hbm, hbm, vmem, vmem, vmem],
-        out_specs=[hbm, hbm, vmem],
-        out_shape=[
-            jax.ShapeDtypeStruct((rhs_count, seg_count, 2, freq_block, freq_width), jnp.float32),
-            jax.ShapeDtypeStruct((seg_count, 2, freq_block, freq_width), jnp.float32),
-            jax.ShapeDtypeStruct((mix_step, freq_width), jnp.float32),
-        ],
-        scratch_shapes=[
-            pltpu.VMEM((fields, cols_all, row_block), jnp.float32),
-            pltpu.VMEM((fields, rows_all, cols_all), jnp.float32),
-            pltpu.VMEM((8, 2 * freq_block, 2 * rows_all), jnp.bfloat16),
-            pltpu.VMEM((8, 2 * freq_block, 2 * rows_all), jnp.bfloat16),
-            pltpu.VMEM((2 * rows_all, freq_width), jnp.bfloat16),
-            pltpu.VMEM((2 * rows_all, freq_width), jnp.bfloat16),
-            pltpu.VMEM((2, 8, 2, freq_block, freq_width), jnp.float32),
-            dma((fields, 8)), dma((fields,)), hops, hops, hops, hops, dma((fields, 8)), dma((fields, 8)),
-        ] + mix_scratch(symbol, seg_count, mix_step),
-        compiler_params=pltpu.CompilerParams(
-            collective_id=0, has_side_effects=True, vmem_limit_bytes=VMEM_LIMIT
-        ),
-        name="forward",
-    )(packed, symbol, fine, coarse, to_cols)
-
-
-def backward_call(symbol, spectra, mixed, norms, curve, fine, coarse, to_cols, line, row_block, col_block):
-    rhs_count, seg_count, _, freq_block, freq_width = spectra.shape
-    mix_step = curve.shape[0]
-    sums_shape = (2,) + norms.shape
-    pair = seg_count // 8
-    fields = rhs_count * pair
-    rows_all, cols_all = row_block * line, col_block * 8
-
-    def body(symbol, spectra, mixed, norms, curve, fine, coarse, to_cols, image, totals, mixed_last,
-             got, part_sum, high, low,
-             half_high, half_low, up_in, down_in, turned, scalars, line_sums, line_total, plane_sums, curve_last,
-             in_send, in_recv, up_send, up_recv, down_send, down_recv, out_send, out_recv,
-             line_send, line_recv, plane_send, plane_recv, *mix_refs):
-        here = Place(line)
-        at = here.at
-        here.greet()
-
-        def enter(last, j, turn):
-            f = last * pair + j
-            src = (mixed_last if last else mixed).at[here.peers[turn] * pair + j]
-            dst = got.at[f, turn]
-            if turn == 0:
-                return pltpu.make_async_copy(src, dst, in_recv.at[f, 0])
-            return send(src, dst, in_send.at[f, turn], in_recv.at[f, turn], at, here.peers[turn])
-
-        def along_line(hops):
-            return send(scalars, line_sums.at[hops], line_send.at[hops], line_recv.at[hops],
-                        here.along(hops), here.me)
-
-        def in_plane(turn):
-            return send(line_total, plane_sums.at[turn], plane_send.at[turn], plane_recv.at[turn],
-                        at, here.peers[turn])
-
-        def begin(last):
-            for j in range(pair):
-                for turn in TURNS:
-                    enter(last, j, turn).start()
-
-        begin(0)
-
-        def build(turn, carry):
-            cos_c, sin_c = coarse[0, pl.ds(turn, 1), :], coarse[1, pl.ds(turn, 1), :]
-            cos_f, sin_f = fine[0], fine[1]
-            cos = split((cos_c * cos_f - sin_c * sin_f).T)
-            sin = split((sin_c * cos_f + cos_c * sin_f).T)
-            for part, table in ((0, high), (1, low)):
-                for half in range(2):
-                    lanes = rows_of(turn * 2 + half, freq_block)
-                    table[:rows_all, lanes] = -sin[part] if half else cos[part]
-                    table[rows_all:, lanes] = cos[part] if half else sin[part]
-            return carry
-
-        mix_one(symbol, spectra.at[rhs_count - 1], mixed_last, curve_last, mix_refs)
-        begin(1)
-        scalars[0] = norms[...]
-        for k, part in ((0, curve), (1, curve_last)):
-            whole = jnp.sum(jnp.sum(part[...], axis=0, keepdims=True), axis=1, keepdims=True)
-            scalars[1, k : k + 1, :] = jnp.broadcast_to(whole, (1, norms.shape[1]))
-        lax.fori_loop(0, 8, build, 0)
-        for hops in range(1, line):
-            along_line(hops).start()
-        total = scalars[...]
-        for hops in range(1, line):
-            along_line(hops).wait()
-            total = total + line_sums[hops]
-        line_total[...] = total
-
-        def block(f, owner):
-            return part_sum.at[f, rows_of(owner, row_block)]
-
-        def up(f, owner):
-            return send(block(f, owner), up_in.at[f, owner - 1], up_send.at[f, owner - 1],
-                        up_recv.at[f, owner - 1], here.along(1), here.me)
-
-        def down(f, owner):
-            return send(block(f, owner), down_in.at[f, owner], down_send.at[f, owner],
-                        down_recv.at[f, owner], here.along(line - 1), here.me)
-
-        def add(f, owner, extra):
-            rows = rows_of(owner, row_block)
-            part_sum[f, rows] = part_sum[f, rows] + extra
-
-        def up_add(f, owner):
-            arrived(up_in.at[f, owner - 1], up_recv.at[f, owner - 1])
-            add(f, owner, up_in[f, owner - 1])
-
-        def down_add(f, owner):
-            arrived(down_in.at[f, owner], down_recv.at[f, owner])
-            add(f, owner, down_in[f, owner])
-
-        def compute(f):
-            for turn in range(8):
-                arrived(got.at[f, turn], in_recv.at[f, turn])
-            spectrum = split(got[f].reshape(16 * freq_block, freq_width))
-            half = product((high[...], low[...]), spectrum)
-            for part in range(2):
-                lanes = slice(part * freq_width, (part + 1) * freq_width)
-                half_high[:, lanes], half_low[:, lanes] = split(half[part * rows_all : (part + 1) * rows_all])
-            part_sum[f] = product_across((half_high[...], half_low[...]), (to_cols[0], to_cols[1]))
-
-        def relay(f, hop):
-            high_end, low_end = line - hop, hop - 1
-
-            @pl.when((at > 0) & (at < high_end))
-            def _():
-                up_add(f, high_end)
-
-            @pl.when(at < high_end)
-            def _():
-                up(f, high_end).start()
-
-            @pl.when((at < line - 1) & (at > low_end))
-            def _():
-                down_add(f, low_end)
-
-            @pl.when(at > low_end)
-            def _():
-                down(f, low_end).start()
-
-        def leave(f, turn):
-            k, j = f // pair, f % pair
-            src = turned.at[f, rows_of(here.peers[turn], col_block)]
-            dst = image.at[k, here.me * pair + j]
-            if turn == 0:
-                return pltpu.make_async_copy(src, dst, out_send.at[f, 0])
-            return send(src, dst, out_send.at[f, turn], out_recv.at[f, turn], at, here.peers[turn])
-
-        def final(f):
-            @pl.when(at > 0)
-            def _():
-                up_add(f, at)
-
-            @pl.when(at < line - 1)
-            def _():
-                down_add(f, at)
-
-            turned[f] = part_sum[f, rows_of(at, row_block)].T
-            for turn in TURNS:
-                leave(f, turn).start()
-
-        for turn in range(1, 8):
-            in_plane(turn).start()
-
-        def step(f, carry):
-            @pl.when(f < fields)
-            def _():
-                compute(f)
-                relay(f, 1)
-
-            @pl.when(f > 0)
-            def _():
-                final(f - 1)
-
-            @pl.when(f < fields)
-            def _():
-                for hop in range(2, line):
-                    relay(f, hop)
-
-            return carry
-
-        lax.fori_loop(0, fields + 1, step, 0)
-        total = line_total[...]
-        for turn in range(1, 8):
-            in_plane(turn).wait()
-            total = total + plane_sums[turn]
-        totals[...] = total
-
-        def finish(f, carry):
-            leave(f, 0).wait()
-            for turn in range(1, 8):
-                leave(f, turn).wait()
-            for owner in range(line):
-                if owner > 0:
-                    @pl.when(at < owner)
-                    def _():
-                        up(f, owner).wait_send()
-
-                if owner < line - 1:
-                    @pl.when(at > owner)
-                    def _():
-                        down(f, owner).wait_send()
-            return carry
-
-        lax.fori_loop(0, fields, finish, 0)
-        for last in range(2):
-            for j in range(pair):
-                for turn in range(1, 8):
-                    enter(last, j, turn).wait_send()
+        done()
 
     dma = pltpu.SemaphoreType.DMA
     vmem = pl.BlockSpec(memory_space=pltpu.VMEM)
     hbm = pl.BlockSpec(memory_space=pl.ANY)
     hops = dma((fields, line - 1))
     stream = pltpu.VMEM((fields, line - 1, row_block, cols_all), jnp.float32)
+    sums_shape = (2,) + norms.shape
+    mixture = jax.ShapeDtypeStruct((seg_count, 2, freq_block, freq_width), jnp.float32)
+    table = pltpu.VMEM((8, 2 * freq_block, 2 * rows_all), jnp.bfloat16)
+    back_table = pltpu.VMEM((2 * rows_all, 16 * freq_block), jnp.bfloat16)
+    half = pltpu.VMEM((2 * rows_all, freq_width), jnp.bfloat16)
+    back_half = pltpu.VMEM((rows_all, 2 * freq_width), jnp.bfloat16)
+    plane = pltpu.VMEM((fields, cols_all, row_block), jnp.float32)
+    pixels = pltpu.VMEM((fields, rows_all, cols_all), jnp.float32)
+    curves = pltpu.VMEM((mix_step, freq_width), jnp.float32)
+    peers = dma((fields, 8))
+    forward_scratch = [
+        plane, pixels, table, table, half, half,
+        pltpu.VMEM((2, 8, 2, freq_block, freq_width), jnp.float32), curves, curves,
+        peers, dma((fields,)), hops, hops, hops, hops, peers, peers,
+    ]
+    backward_scratch = [
+        pltpu.VMEM((fields, 8, 2, freq_block, freq_width), jnp.float32),
+        pixels, back_table, back_table, back_half, back_half, stream, stream, plane,
+        pltpu.VMEM(sums_shape, jnp.float32),
+        pltpu.VMEM((line,) + sums_shape, jnp.float32),
+        pltpu.VMEM(sums_shape, jnp.float32),
+        pltpu.VMEM((8,) + sums_shape, jnp.float32),
+        peers, peers, hops, hops, hops, hops, peers, peers,
+        dma((line,)), dma((line,)), dma((8,)), dma((8,)),
+    ]
     return pl.pallas_call(
         body,
-        in_specs=[hbm, hbm, hbm, vmem, vmem, vmem, vmem, vmem],
-        out_specs=[hbm, vmem, hbm],
+        in_specs=[hbm, hbm, vmem, vmem, vmem, vmem],
+        out_specs=[hbm, vmem, hbm, hbm, hbm],
         out_shape=[
-            jax.ShapeDtypeStruct((rhs_count, seg_count, col_block, row_block), jnp.float32),
+            jax.ShapeDtypeStruct(packed.shape, jnp.float32),
             jax.ShapeDtypeStruct(sums_shape, jnp.float32),
-            jax.ShapeDtypeStruct(mixed.shape, jnp.float32),
+            jax.ShapeDtypeStruct((rhs_count,) + mixture.shape, jnp.float32),
+            mixture, mixture,
         ],
-        scratch_shapes=[
-            pltpu.VMEM((fields, 8, 2, freq_block, freq_width), jnp.float32),
-            pltpu.VMEM((fields, rows_all, cols_all), jnp.float32),
-            pltpu.VMEM((2 * rows_all, 16 * freq_block), jnp.bfloat16),
-            pltpu.VMEM((2 * rows_all, 16 * freq_block), jnp.bfloat16),
-            pltpu.VMEM((rows_all, 2 * freq_width), jnp.bfloat16),
-            pltpu.VMEM((rows_all, 2 * freq_width), jnp.bfloat16),
-            stream, stream,
-            pltpu.VMEM((fields, cols_all, row_block), jnp.float32),
-            pltpu.VMEM(sums_shape, jnp.float32),
-            pltpu.VMEM((line,) + sums_shape, jnp.float32),
-            pltpu.VMEM(sums_shape, jnp.float32),
-            pltpu.VMEM((8,) + sums_shape, jnp.float32),
-            pltpu.VMEM(curve.shape, jnp.float32),
-            dma((fields, 8)), dma((fields, 8)), hops, hops, hops, hops, dma((fields, 8)), dma((fields, 8)),
-            dma((line,)), dma((line,)), dma((8,)), dma((8,)),
-        ] + mix_scratch(symbol, seg_count, mix_step),
+        scratch_shapes=forward_scratch + mix_scratch(symbol, seg_count, mix_step) + backward_scratch,
         compiler_params=pltpu.CompilerParams(
-            collective_id=1, has_side_effects=True, vmem_limit_bytes=VMEM_LIMIT
+            collective_id=0, has_side_effects=True, vmem_limit_bytes=VMEM_LIMIT
         ),
-        name="backward",
-    )(symbol, spectra, mixed, norms, curve, fine, coarse, to_cols)
+        name="operate",
+    )(packed, symbol, norms, fine, coarse, to_cols)
 
 
 def halves(table):
@@ -712,10 +700,8 @@
     norm_now = jnp.sum(right_side * right_side, axis=(1, 2, 3))
     norms = jnp.broadcast_to(norm_now[:, None], (rhs_count, 128))
     to_cols = halves(to_cols.transpose(1, 0, 2).reshape(cols_all, 2 * freq_width))
-    spectra, mixed, curve = forward_call(right_side.transpose(0, 1, 3, 2), symbol, fine, coarse, to_cols, line)
-    image, totals, _ = backward_call(
-        symbol, spectra, mixed, norms, curve, fine, coarse, to_cols, line, row_block, col_block
-    )
+    packed = right_side.transpose(0, 1, 3, 2)
+    image, totals, _, _, _ = operate_call(packed, symbol, norms, fine, coarse, to_cols, line)
     applied = image.transpose(0, 1, 3, 2) * norm_factor
     step_size = (totals[0, :, 0] / (totals[1, :, 0] * norm_factor))[:, None, None, None]
     return (step_size * right_side, right_side - step_size * applied)
@@ -726,7 +712,7 @@
     rhs_count, seg_count, rows, cols = right_side.shape
     freq_rows, freq_cols = symbol.shape[:2]
     aligned = all(n % 128 == 0 for n in (rows // ring, freq_rows // wide, freq_cols // ring))
-    return ring > 1 and wide == 8 and rhs_count == 2 and seg_count % 8 == 0 and cols // wide % 8 == 0 and aligned
+    return ring > 1 and wide == 8 and rhs_count == 2 and seg_count % 16 == 0 and cols // wide % 8 == 0 and aligned
 
 
 def solution(mesh):

time: 281 us -> 274 us (0.975)
  Pallas kernels: 267 us -> 260 us
    pallas_call x2 -> x1, Pallas kernels: 267 us -> 260 us  [operate_call(): pl.pallas_call(body, in_specs=[hbm, hbm, vmem, vmem, vmem, vmem], out_spe...]
where the time goes in v3:
time: 274 us; the launch traced here: 273 us
  Pallas kernels  260 us (95%)
  other arithmetic  10.5 us (4%)
    pallas_call x1, Pallas kernels, operate_call(): pl.pallas_call(body, in_specs=[hbm, hbm, vmem, vmem, vmem, vmem], out_spe...  260 us

profile of v3, /device:TPU:0, one launch (start us, length us, event | category | flops | bytes accessed | tf_op | source)
XLA Modules:
  0.0 273.2 jit_solution(14638483402443338815)
XLA Ops:
  0.7 0.1 stack.62
  0.8 1.5 multiply_reduce_fusion
  2.2 0.6 broadcast_in_dim.2.norms
  2.9 0.2 fusion.23
  3.1 0.6 pad_maximum_fusion.2.coarse
  3.7 0.6 fusion.21
  4.3 0.2 fusion.19
  4.6 0.6 fusion.1
  5.2 0.8 reshape.98
  6.0 0.2 reduce-precision_convert_fusion
  6.2 1.1 pad_maximum_fusion.to_cols
  7.3 1.0 fusion.8
  8.3 0.8 pad_maximum_fusion.1.fine
  9.1 0.0 copy-start
  9.1 260.2 %operate.1 = (f32[2,16,64,128]{3,2,1,0:T(8,128)}, f32[2,2,128]{2,1,0:T(2,128)}, f32[2,16,2,128,256]{4,3,2,1,0:T(8,128)}, f32[16,2,128,256]{3,2,1,0:T(8,128)}, f32[16,2,128,256]{3,2,1,0:T(8,128)}) custom-call(f32[2,16,64,128]{3,2,1,0:T(8,128)} %bitcast.26, f32[128,256,256]{2,1,0:T(8,128)} %symbol.1, f32[2,128]{1,0:T(2,128)} %broadcast_in_dim.2.norms, ...), custom_call_target="tpu_custom_call" | custom-call | tf_op jit(solution)/shard_map/operate/pallas_call | solution.py:666
  269.4 0.8 fusion.25
  270.2 0.0 copy-done
  270.2 3.0 %bitcast_subtract_fusion = (f32[2,16,128,64]{2,3,1,0:T(8,128)}, f32[2,16,128,64]{2,3,1,0:T(8,128)}) fusion(f32[2,16,128,64]{2,3,1,0:T(8,128)S(1)} %copy-done, f32[2,16,64,128]{3,2,1,0:T(8,128)} %get-tuple-element.21, f32[2]{0:T(128)S(1)} %broadcast_multiply_fusion.1, f32[2]{0:T(128)S(1)} %fusion.25), kind=kLoop, calls=%fused_computation.4 | loop fusion | flops 786432 | bytes 4194320 | tf_op jit(solution)/shard_map/sub | solution.py:707
  (8 shorter events, 0.1 us)
Async XLA Ops:
  9.1 261.0 %copy-start = (f32[2,16,128,64]{2,3,1,0:T(8,128)S(1)}, f32[2,16,128,64]{2,3,1,0:T(8,128)}, u32[]{:S(2)}) copy-start(f32[2,16,128,64]{2,3,1,0:T(8,128)} %param.2) | copy-start | bytes 3145732
